TPU v7x, 128 devices: a whole 4x4x4 slice. The times are simulated.
128 devices in a mesh: rep: 32 (over z, x, core), tp: 4 (over y).
Axes of the slice: x: 4, y: 4, z: 4, core: 2. Of those that a mesh axis runs over, the one named last changes fastest.
Arguments:
- hidden_in: bfloat16 [4096, 2048], P('rep'), may hold values from -6 to 6
- new_lengths: int32 [32, 4], P('rep'), may hold values from 1 to 64, 128 in all within a row
- prefix_lengths: int32 [32, 4], P('rep'), may hold values from 1 to 512, 1024 in all within a row
- cache_keys: bfloat16 [32768, 2048], P('rep', 'tp'), may hold values from -6 to 6
- cache_values: bfloat16 [32768, 2048], P('rep', 'tp'), may hold values from -6 to 6
- attn_gain: float32 [2048], replicated, may hold values from 0.1 to 1.9
- w_qkv: bfloat16 [2048, 3, 2048], P(None, None, 'tp'), may hold values from -1 to 1
- norm_gains: float32 [2, 2048], P(None, 'tp'), may hold values from 0 to 11
- w_out: bfloat16 [2048, 2048], P('tp'), may hold values from -0.125 to 0.125
- moe_gain: float32 [2048], replicated, may hold values from 0.1 to 1.9
- expert_ids: int32 [4096, 8], P('rep'), may hold values from 0 to 63, all different within a row; in each aligned block of 32 rows (0 to 31, 32 to 63, ...) at most 6 rows name the same one
- expert_weights: float32 [4096, 8], P('rep'), may hold values from 0.05 to 0.5
- w_gate_up: bfloat16 [64, 2048, 2, 1024], P('rep', None, None, 'tp'), may hold values from -0.125 to 0.125
- w_down: bfloat16 [64, 1024, 2048], P('rep', 'tp'), may hold values from -0.1875 to 0.1875
- next_gain: float32 [2048], replicated, may hold values from 0.1 to 1.9
- next_qkv: bfloat16 [2048, 3, 2048], P(None, None, 'tp'), may hold values from -1 to 1
- next_norm_gains: float32 [2, 2048], P(None, 'tp'), may hold values from 0.1 to 1.9
Outputs:
- hidden_out: bfloat16 [4096, 2048], P('rep')
- next_qkv_out: bfloat16 [4096, 3, 2048], P('rep', None, 'tp')
Inputs may be any that keep to these rules, and one draw needn't show every extreme that they name: `expert_ids`: in every aligned block of 32 tokens no expert is chosen more than 6 times, and some block reaches 6; a token's 8 experts differ. `new_lengths`: each replica's lengths sum to 128; its longest request has exactly 64 new tokens. `prefix_lengths`: each replica's prefix lengths sum to 1024; its longest prefix has exactly 512 tokens.
All inputs are finite; a program needn't handle non-finite values.
Results may differ from a plain program's by a relative error of at most 0.023.
Values may be sent and summed in bfloat16 or wider, within the bound.
A program may use at most 128 MiB of HBM per device.

v0:
```python
import math

import jax
import jax.numpy as jnp
from jax import lax
from jax.sharding import PartitionSpec as P

HD = 128


eps_norm = 1e-05
eps_head = 1e-06
rope_base = 10000.0


def rms_scale(inputs, gain):
    inputs = inputs.astype(jnp.float32)
    scaled = inputs * lax.rsqrt(jnp.mean(inputs * inputs, axis=-1, keepdims=True) + eps_norm)
    return (scaled * gain).astype(jnp.bfloat16)


def request_tables(new_lengths, prefix_lengths, row_count, cache_count):
    new_end = jnp.cumsum(new_lengths, dtype=jnp.int32)
    cache_end = jnp.cumsum(prefix_lengths, dtype=jnp.int32)
    token_index = jnp.arange(row_count, dtype=jnp.int32)
    cache_index = jnp.arange(cache_count, dtype=jnp.int32)
    token_request = jnp.sum(
        (token_index[:, None] >= new_end[None, :]).astype(jnp.int32), axis=1, dtype=jnp.int32
    )
    cache_request = jnp.sum(
        (cache_index[:, None] >= cache_end[None, :]).astype(jnp.int32), axis=1, dtype=jnp.int32
    )
    requests = new_lengths.shape[0]
    selector = token_request[:, None] == jnp.arange(requests, dtype=jnp.int32)[None, :]
    new_start = new_end - new_lengths
    offset = token_index - jnp.sum(
        jnp.where(selector, new_start[None, :], 0), axis=1, dtype=jnp.int32
    )
    position = offset + jnp.sum(
        jnp.where(selector, prefix_lengths[None, :], 0), axis=1, dtype=jnp.int32
    )
    return (token_request, cache_request, position)


def project_heads(normed, weight, gains, position, head_size):
    row_count = normed.shape[0]
    proj_width = weight.shape[2]
    full_width = proj_width * lax.axis_size("tp")
    projected = jnp.dot(
        normed, weight.reshape(weight.shape[0], 3 * proj_width), preferred_element_type=jnp.float32
    )
    projected = projected.reshape(row_count, 3, proj_width)
    squares = jnp.sum(projected[:, :2, :] * projected[:, :2, :], axis=2)
    totals = lax.psum(squares, "tp")
    inverse = lax.rsqrt(totals / full_width + eps_head)
    head_count = proj_width // head_size
    half_size = head_size // 2
    frequency = rope_base ** (-jnp.arange(half_size, dtype=jnp.float32) * 2.0 / head_size)
    angles = position.astype(jnp.float32)[:, None] * frequency[None, :]
    cosine = jnp.cos(angles)[:, None, :]
    sine_table = jnp.sin(angles)[:, None, :]
    outputs = []
    for member in range(2):
        member_rows = projected[:, member, :] * inverse[:, member : member + 1]
        portion = (member_rows * gains[member][None, :]).reshape(row_count, head_count, head_size)
        lower_half = portion[..., :half_size]
        upper_half = portion[..., half_size:]
        turned = jnp.concatenate(
            [
                lower_half * cosine - upper_half * sine_table,
                upper_half * cosine + lower_half * sine_table,
            ],
            axis=-1,
        )
        outputs.append(turned.reshape(row_count, proj_width).astype(jnp.bfloat16))
    outputs.append(projected[:, 2, :].astype(jnp.bfloat16))
    return jnp.stack(outputs, axis=1)


def attend(qkv, key_cache, value_cache, token_request, cache_request, head_size):
    row_count = qkv.shape[0]
    proj_width = qkv.shape[2]
    head_count = proj_width // head_size
    queries = qkv[:, 0, :].reshape(row_count, head_count, head_size)
    key_rows = jnp.concatenate([key_cache, qkv[:, 1, :]], axis=0).reshape(-1, head_count, head_size)
    value_rows = jnp.concatenate([value_cache, qkv[:, 2, :]], axis=0).reshape(
        -1, head_count, head_size
    )
    scores = jnp.einsum(
        "qhd,khd->hqk", queries, key_rows, preferred_element_type=jnp.float32
    ) / math.sqrt(head_size)
    token_index = jnp.arange(row_count, dtype=jnp.int32)
    cache_ok = cache_request[None, :] == token_request[:, None]
    new_ok = (token_request[None, :] == token_request[:, None]) & (
        token_index[None, :] <= token_index[:, None]
    )
    allowed = jnp.concatenate([cache_ok, new_ok], axis=1)
    scores = jnp.where(allowed[None], scores, -1e30)
    row_max = jnp.max(scores, axis=-1, keepdims=True)
    weights = jnp.exp(scores - row_max)
    weights = (weights / jnp.sum(weights, axis=-1, keepdims=True)).astype(jnp.bfloat16)
    context = jnp.einsum("hqk,khd->qhd", weights, value_rows, preferred_element_type=jnp.float32)
    return context.reshape(row_count, proj_width).astype(jnp.bfloat16)


def slot_ranks(expert_rows, expert_count):
    onehot = (
        expert_rows[:, :, None] == jnp.arange(expert_count, dtype=jnp.int32)[None, None, :]
    ).astype(jnp.int32)
    before = jnp.cumsum(onehot, axis=1, dtype=jnp.int32) - onehot
    return jnp.sum(before * onehot, axis=2, dtype=jnp.int32)


def expert_rows(received, w_gate_up, w_down):
    sources, local_count, slot_count, model_width = received.shape
    hidden_size = w_gate_up.shape[3]
    results = []
    for expert_slot in range(local_count):
        gathered = received[:, expert_slot].reshape(sources * slot_count, model_width)
        gate_up_out = jnp.dot(
            gathered,
            w_gate_up[expert_slot].reshape(model_width, 2 * hidden_size),
            preferred_element_type=jnp.float32,
        )
        activated = (
            jax.nn.silu(gate_up_out[:, :hidden_size]) * gate_up_out[:, hidden_size:]
        ).astype(jnp.bfloat16)
        portion = jnp.dot(
            activated, w_down[expert_slot], preferred_element_type=jnp.float32
        ).astype(jnp.bfloat16)
        results.append(portion.reshape(sources, slot_count, model_width))
    return jnp.stack(results, axis=1)


def per_device(
    hidden_in,
    new_lengths,
    prefix_lengths,
    cache_keys,
    cache_values,
    attn_gain,
    w_qkv,
    norm_gains,
    w_out,
    moe_gain,
    expert_ids,
    expert_weights,
    w_gate_up,
    w_down,
    next_gain,
    next_qkv,
    next_norm_gains,
):
    row_count, model_width = hidden_in.shape
    cache_count = cache_keys.shape[0]
    tp_count = lax.axis_size("tp")
    rep_count = lax.axis_size("rep")
    choose_count = expert_ids.shape[1]
    local_count = w_gate_up.shape[0]
    expert_count = local_count * rep_count
    quarter = row_count // tp_count
    slot_cap = max(2, quarter * choose_count * 3 // (2 * expert_count))
    full_cap = tp_count * slot_cap
    token_request, cache_request, position = request_tables(
        new_lengths[0], prefix_lengths[0], row_count, cache_count
    )
    normed = rms_scale(hidden_in, attn_gain)
    qkv = project_heads(normed, w_qkv, norm_gains, position, HD)
    context = attend(qkv, cache_keys, cache_values, token_request, cache_request, HD)
    attn_part = jnp.dot(context, w_out, preferred_element_type=jnp.float32)
    attn_out = lax.psum(attn_part.astype(jnp.bfloat16), "tp").astype(jnp.float32)
    mid_stream = (hidden_in.astype(jnp.float32) + attn_out).astype(jnp.bfloat16)
    moe_input = rms_scale(mid_stream, moe_gain)
    rank_of = slot_ranks(
        expert_ids.reshape(tp_count, quarter * choose_count), expert_count
    ).reshape(-1)
    ids_flat = expert_ids.reshape(-1)
    entry = jnp.arange(row_count * choose_count, dtype=jnp.int32)
    quarter_of = entry // (quarter * choose_count)
    flat_slot = ids_flat * full_cap + quarter_of * slot_cap + rank_of
    slot_table = (
        jnp.full((expert_count * full_cap,), row_count, jnp.int32)
        .at[flat_slot]
        .set(entry // choose_count)
    )
    padded = jnp.concatenate([moe_input, jnp.zeros((1, model_width), jnp.bfloat16)], axis=0)
    outgoing = padded[slot_table].reshape(rep_count, local_count, full_cap, model_width)
    produced = expert_rows(
        lax.all_to_all(outgoing, "rep", split_axis=0, concat_axis=0, tiled=True), w_gate_up, w_down
    )
    returned = lax.all_to_all(produced, "rep", split_axis=0, concat_axis=0, tiled=True)
    picked = returned.reshape(expert_count * full_cap, model_width)[flat_slot].astype(jnp.float32)
    partial_value = jnp.sum(
        picked.reshape(row_count, choose_count, model_width) * expert_weights[:, :, None], axis=1
    )
    moe_out = lax.psum(partial_value.astype(jnp.bfloat16), "tp").astype(jnp.float32)
    hidden_out = (mid_stream.astype(jnp.float32) + moe_out).astype(jnp.bfloat16)
    next_input = rms_scale(hidden_out, next_gain)
    next_qkv_out = project_heads(next_input, next_qkv, next_norm_gains, position, HD)
    return (hidden_out, next_qkv_out)


def solution(mesh):
    placed = (
        P("rep", None),
        P("rep", None),
        P("rep", None),
        P("rep", "tp"),
        P("rep", "tp"),
        P(),
        P(None, None, "tp"),
        P(None, "tp"),
        P("tp", None),
        P(),
        P("rep", None),
        P("rep", None),
        P("rep", None, None, "tp"),
        P("rep", "tp", None),
        P(),
        P(None, None, "tp"),
        P(None, "tp"),
    )
    return jax.shard_map(
        per_device,
        mesh=mesh,
        in_specs=placed,
        out_specs=(P("rep", None), P("rep", None, "tp")),
        check_vma=False,
    )
```

profile of v0, /device:TPU:1, one launch (start us, length us, event | category | flops | bytes accessed | tf_op | source)
XLA Modules:
  0.0 370.0 jit_solution(4477578113990545724)
XLA Ops:
  7.2 9.0 %copy.73 = bf16[2048,3,512]{0,2,1:T(8,128)(2,1)} copy(bf16[2048,3,512]{2,0,1:T(8,128)(2,1)} %param.23) | data formatting | bytes 12582912 | tf_op args[6]
  16.2 0.2 fusion.14
  16.4 5.0 %fusion.4 = f32[128,3,512]{2,0,1:T(8,128)S(1)} fusion(bf16[2048,3,512]{0,2,1:T(8,128)(2,1)} %copy.73, bf16[128,2048]{1,0:T(8,128)(2,1)S(1)} %copy-done.2, f32[2048]{0:T(1024)S(1)} %copy-done.9, f32[128]{0:T(128)S(1)} %add_rsqrt_fusion.4), kind=kOutput, calls=%fused_computation.9 | convolution fusion | flops 806354944 | bytes 7610880 | tf_op jit(solution)/shard_map/dot_general | solution.py:49
  21.5 0.1 fusion.33
  21.6 0.5 multiply_power_fusion
  22.4 9.6 %psum.28 = f32[128,2]{0,1:T(2,128)S(1)} all-reduce(f32[128,2]{0,1:T(2,128)S(1)} %fusion.33), channel_id=1, replica_groups=mesh['rep'=32,'tp'=4] {'tp'}, use_global_device_ids=true, to_apply=%region_6.7 | all-reduce | flops 256 | bytes 2048 | tf_op jit(solution)/shard_map/psum | solution.py:54
  32.0 0.2 reduce-window.24
  32.4 0.7 select_reduce_fusion.1
  33.1 1.0 multiply_cosine_fusion
  34.1 0.1 fusion.45
  34.2 0.9 subtract_convert_fusion.3
  35.2 0.1 copy.77
  35.3 2.3 copy.78
  37.6 0.2 reduce-window.19
  37.9 0.1 broadcast_compare_fusion
  38.1 2.3 pad_maximum_fusion.1
  40.4 2.4 copy.74
  42.8 2.3 pad_maximum_fusion.2
  45.1 3.7 fusion.83
  48.8 2.6 fusion.10
  51.5 1.3 convolution_convert_fusion.2
  53.1 2.4 reduce-window.25
  55.5 0.1 slice.160
  55.7 0.1 copy.83
  55.8 0.2 fusion.44
  56.2 4.3 %scatter_custom_fusion = s32[1536]{0:T(1024)S(1)} fusion(s32[1024]{0:T(1024)S(1)} %bitcast.137, s32[1024]{0:T(1024)S(1)} %add_select_fusion, s32[]{:T(128)} %constant.74.clone.1), kind=kCustom, calls=%fused_computation.120 | custom fusion | bytes 6148 | tf_op jit(solution)/shard_map/scatter | solution.py:184
  60.6 35.4 %all-reduce.4.cloned.1.call-done = bf16[128,2048]{1,0:T(8,128)(2,1)} async-done(((bf16[128,2048]{1,0:T(8,128)(2,1)}), bf16[128,2048]{1,0:T(8,128)(2,1)}) %all-reduce.4.cloned.1.call-update) | async-done | bytes 524304 | tf_op jit(solution)/shard_map/psum | solution.py:171
  95.9 1.3 fusion.18
  97.3 1.3 fusion.20
  98.6 7.1 %gather_fusion = bf16[1536,2048]{1,0:T(8,128)(2,1)} fusion(bf16[129,2048]{1,0:T(8,128)(2,1)S(1)} %concatenate.33, s32[2048]{0:T(1024)S(1)} %pad_clamp_fusion), kind=kCustom, calls=%fused_computation | custom fusion | bytes 12589056 | tf_op jit(solution)/shard_map/gather | solution.py:187
  105.7 9.7 %all-to-all-start = ((bf16[32,2,24,2048]{3,2,1,0:T(8,128)(2,1)}), bf16[32,2,24,2048]{3,2,1,0:T(8,128)(2,1)}, u32[]{:S(2)}, u32[]{:S(2)}) async-start(bf16[32,2,24,2048]{3,2,1,0:T(8,128)(2,1)} %bitcast.119), calls=%async_computation | async-start | bytes 12582912 | tf_op jit(solution)/shard_map/all_to_all | solution.py:189
  115.4 4.7 %fusion.78 = (bf16[1,2048,2,256]{3,2,1,0:T(2,128)(2,1)S(1)}, bf16[1,2048,2,256]{3,2,1,0:T(2,128)(2,1)S(1)}) fusion(bf16[2,2048,2,256]{3,2,1,0:T(2,128)(2,1)} %param.29), kind=kLoop, calls=%fused_computation.151 | loop fusion | bytes 8388608 | tf_op jit(solution)/shard_map/slice | solution.py:122
  120.1 1.9 copy.101
  122.0 1.8 copy.102
  123.8 64.6 %all-to-all-done = bf16[32,2,24,2048]{3,2,1,0:T(8,128)(2,1)} async-done(((bf16[32,2,24,2048]{3,2,1,0:T(8,128)(2,1)}), bf16[32,2,24,2048]{3,2,1,0:T(8,128)(2,1)}, u32[]{:S(2)}, u32[]{:S(2)}) %all-to-all-start) | async-done | bytes 6291488 | tf_op jit(solution)/shard_map/all_to_all | solution.py:189
  188.4 3.4 fusion.77
  191.8 1.8 fusion.86
  193.6 1.0 convolution_convert_fusion.1
  194.6 0.6 copy-done.5
  195.2 1.8 fusion.87
  197.0 1.0 convolution_convert_fusion
  198.0 3.2 pad_maximum_fusion
  201.3 9.8 %all-to-all-start.1 = ((bf16[32,2,24,2048]{3,2,1,0:T(8,128)(2,1)}), bf16[32,2,24,2048]{3,2,1,0:T(8,128)(2,1)}, u32[]{:S(2)}, u32[]{:S(2)}) async-start(bf16[32,2,24,2048]{3,2,1,0:T(8,128)(2,1)} %pad_maximum_fusion), calls=%async_computation.1 | async-start | bytes 12582912 | tf_op jit(solution)/shard_map/all_to_all | solution.py:191
  211.1 0.3 all-reduce.6.cloned.1.call-start
  211.5 72.6 %all-to-all-done.1 = bf16[32,2,24,2048]{3,2,1,0:T(8,128)(2,1)} async-done(((bf16[32,2,24,2048]{3,2,1,0:T(8,128)(2,1)}), bf16[32,2,24,2048]{3,2,1,0:T(8,128)(2,1)}, u32[]{:S(2)}, u32[]{:S(2)}) %all-to-all-start.1) | async-done | bytes 6291488 | tf_op jit(solution)/shard_map/all_to_all | solution.py:191
  284.1 12.4 %gather_fusion.1 = bf16[1024,2048]{1,0:T(8,128)(2,1)} fusion(bf16[1536,2048]{1,0:T(8,128)(2,1)} %bitcast.33, s32[1024]{0:T(1024)S(1)} %broadcast_clamp_fusion), kind=kCustom, calls=%fused_computation.1 | custom fusion | bytes 8392704 | tf_op jit(solution)/shard_map/gather | solution.py:192
  296.5 7.3 %fusion.1 = bf16[128,2048]{1,0:T(8,128)(2,1)} fusion(bf16[1024,2048]{1,0:T(8,128)(2,1)} %gather_fusion.1, f32[128,8]{1,0:T(8,128)S(1)} %copy.88), kind=kLoop, calls=%fused_computation.5 | loop fusion | flops 6029312 | bytes 4722688 | tf_op jit(solution)/shard_map/reduce_sum | solution.py:193
  303.9 8.9 %copy.89 = bf16[2048,3,512]{0,2,1:T(8,128)(2,1)} copy(bf16[2048,3,512]{2,0,1:T(8,128)(2,1)} %param.32) | data formatting | bytes 12582912 | tf_op args[15]
  312.8 32.9 %all-reduce.6.cloned.1.call-done = bf16[128,2048]{1,0:T(8,128)(2,1)} async-done(((bf16[128,2048]{1,0:T(8,128)(2,1)}), bf16[128,2048]{1,0:T(8,128)(2,1)}) %all-reduce.6.cloned.1.call-update) | async-done | bytes 524304 | tf_op jit(solution)/shard_map/psum | solution.py:196
  345.8 1.4 fusion.11
  347.2 5.2 %fusion.2 = f32[128,3,512]{2,0,1:T(8,128)S(1)} fusion(bf16[2048,3,512]{0,2,1:T(8,128)(2,1)} %copy.89, bf16[128,2048]{1,0:T(8,128)(2,1)S(1)} %get-tuple-element.5, f32[2048]{0:T(1024)S(1)} %copy-done.11, f32[128]{0:T(128)S(1)} %add_rsqrt_fusion.2), kind=kOutput, calls=%fused_computation.7 | convolution fusion | flops 806354944 | bytes 7610880 | tf_op jit(solution)/shard_map/dot_general | solution.py:49
  352.4 0.1 fusion.32
  352.6 0.1 copy.93
  352.7 0.1 copy.94
  352.8 8.0 %psum.31 = f32[128,2]{0,1:T(2,128)S(1)} all-reduce(f32[128,2]{0,1:T(2,128)S(1)} %fusion.32), channel_id=1, replica_groups=mesh['rep'=32,'tp'=4] {'tp'}, use_global_device_ids=true, to_apply=%region_21.22 | all-reduce | flops 256 | bytes 2048 | tf_op jit(solution)/shard_map/psum | solution.py:54
  360.9 0.1 copy.90
  361.0 0.1 copy.91
  361.4 0.3 subtract_convert_fusion.1
  361.7 0.1 copy.92
  361.9 0.1 copy.96
  362.0 0.1 pad_maximum_fusion.6
  362.1 0.1 copy.95
  362.3 0.1 copy.97
  362.4 0.8 pad_maximum_fusion.3
  (85 shorter events, 1.9 us)
Async XLA Ops:
  7.2 44.3 %copy-start = (bf16[512,2048]{1,0:T(8,128)(2,1)S(1)}, bf16[512,2048]{1,0:T(8,128)(2,1)}, u32[]{:S(2)}) copy-start(bf16[512,2048]{1,0:T(8,128)(2,1)} %param.25) | copy-start | bytes 6291460
  7.2 9.1 %copy-start.2 = (bf16[128,2048]{1,0:T(8,128)(2,1)S(1)}, bf16[128,2048]{1,0:T(8,128)(2,1)}, u32[]{:S(2)}) copy-start(bf16[128,2048]{1,0:T(8,128)(2,1)} %param.17) | copy-start | bytes 1572868
  7.2 9.3 %copy-start.9 = (f32[2048]{0:T(1024)S(1)}, f32[2048]{0:T(1024)}, u32[]{:S(2)}) copy-start(f32[2048]{0:T(1024)} %param.22) | copy-start | bytes 24580
  7.2 88.7 %all-reduce.4.cloned.1.call-start = ((), (), s32[]{:S(2)}) async-start(), calls=%async_computation.2 | async-start | bytes 1048576 | tf_op jit(solution)/shard_map/psum | solution.py:171
  21.5 10.5 %copy-start.15 = (f32[2,512]{1,0:T(2,128)S(1)}, f32[2,512]{1,0:T(2,128)}, u32[]{:S(2)}) copy-start(f32[2,512]{1,0:T(2,128)} %param.24) | copy-start | bytes 12292
  21.5 10.5 %copy-start.19 = (s32[1,4]{1,0:T(1,128)S(1)}, s32[1,4]{1,0:T(1,128)}, u32[]{:S(2)}) copy-start(s32[1,4]{1,0:T(1,128)} %param.18) | copy-start | bytes 52
  32.3 1.9 copy-start.12
  34.2 3.4 copy-start.17
  34.2 3.7 copy-start.13
  40.4 4.7 %copy-start.7 = (bf16[128,4,64]{2,0,1:T(8,128)(2,1)S(1)}, bf16[128,4,64]{2,0,1:T(8,128)(2,1)}, u32[]{:S(2)}) copy-start(bf16[128,4,64]{2,0,1:T(8,128)(2,1)} %get-tuple-element.19) | copy-start | bytes 196612
  51.4 1.3 copy-start.8
  52.7 44.5 %copy-start.10 = (f32[2048]{0:T(1024)S(1)}, f32[2048]{0:T(1024)}, u32[]{:S(2)}) copy-start(f32[2048]{0:T(1024)} %param.26) | copy-start | bytes 24580
  105.7 82.7 %all-to-all-start = ((bf16[32,2,24,2048]{3,2,1,0:T(8,128)(2,1)}), bf16[32,2,24,2048]{3,2,1,0:T(8,128)(2,1)}, u32[]{:S(2)}, u32[]{:S(2)}) async-start(bf16[32,2,24,2048]{3,2,1,0:T(8,128)(2,1)} %bitcast.119), calls=%async_computation | async-start | bytes 12582912 | tf_op jit(solution)/shard_map/all_to_all | solution.py:189
  123.8 68.0 %copy-start.6 = (bf16[256,8,2,256]{3,1,2,0:T(8,128)(2,1)S(1)}, bf16[256,8,2,256]{3,1,2,0:T(8,128)(2,1)}, u32[]{:S(2)}) copy-start(bf16[256,8,2,256]{3,1,2,0:T(8,128)(2,1)} %copy.101) | copy-start | bytes 6291460
  191.8 1.8 copy-start.18
  193.6 1.6 copy-start.5
  201.3 10.1 %copy-start.14 = (f32[128,8]{0,1:T(8,128)S(1)}, f32[128,8]{0,1:T(8,128)}, u32[]{:S(2)}) copy-start(f32[128,8]{0,1:T(8,128)} %param.28) | copy-start | bytes 12292
  201.3 82.9 %all-to-all-start.1 = ((bf16[32,2,24,2048]{3,2,1,0:T(8,128)(2,1)}), bf16[32,2,24,2048]{3,2,1,0:T(8,128)(2,1)}, u32[]{:S(2)}, u32[]{:S(2)}) async-start(bf16[32,2,24,2048]{3,2,1,0:T(8,128)(2,1)} %pad_maximum_fusion), calls=%async_computation.1 | async-start | bytes 12582912 | tf_op jit(solution)/shard_map/all_to_all | solution.py:191
  211.1 134.6 %all-reduce.6.cloned.1.call-start = ((), (), s32[]{:S(2)}) async-start(), calls=%async_computation.3 | async-start | bytes 1048576 | tf_op jit(solution)/shard_map/psum | solution.py:196
  303.9 8.9 %copy-start.16 = (f32[2,512]{1,0:T(2,128)S(1)}, f32[2,512]{1,0:T(2,128)}, u32[]{:S(2)}) copy-start(f32[2,512]{1,0:T(2,128)} %param.33) | copy-start | bytes 12292
  303.9 41.9 %copy-start.3 = (bf16[128,2048]{1,0:T(8,128)(2,1)S(1)}, bf16[128,2048]{1,0:T(8,128)(2,1)}, u32[]{:S(2)}) copy-start(bf16[128,2048]{1,0:T(8,128)(2,1)} %all-reduce.4.cloned.1.call-done) | copy-start | bytes 1572868
  303.9 43.2 %copy-start.11 = (f32[2048]{0:T(1024)S(1)}, f32[2048]{0:T(1024)}, u32[]{:S(2)}) copy-start(f32[2048]{0:T(1024)} %param.31) | copy-start | bytes 24580
  347.1 5.2 %copy-start.4 = (bf16[128,2048]{1,0:T(8,128)(2,1)}, bf16[128,2048]{1,0:T(8,128)(2,1)S(1)}, u32[]{:S(2)}) copy-start(bf16[128,2048]{1,0:T(8,128)(2,1)S(1)} %get-tuple-element.5) | copy-start | bytes 1572868
  361.3 1.9 copy-start.1
Sparse Core Ops, SparseCore 0:
  52.9 43.0 all-reduce.3
  304.0 41.6 all-reduce.5
where the time goes:
time: 374 us; the launch traced here: 370 us
  waiting for transfers between devices  206 us (55%)
  local copies, waits for them, and re-layouts  61.2 us (16%)
  other arithmetic  27.7 us (7%)
  matrix products  23.4 us (6%)
  starting transfers between devices  19.9 us (5%)
  blocking collectives  17.6 us (5%)
  between operations  14.6 us (4%)
    all_to_all x1, waiting for transfers between devices, per_device(): lax.all_to_all(produced, 'rep', split_axis=0, concat_axis=0, tiled=True)  72.6 us
    all_to_all x1, waiting for transfers between devices, per_device(): lax.all_to_all(outgoing, 'rep', split_axis=0, concat_axis=0, tiled=True)  64.6 us
    psum x1, waiting for transfers between devices, per_device(): lax.psum(attn_part.astype(jnp.bfloat16), 'tp').astype(jnp.float32)  35.4 us
    psum x1, waiting for transfers between devices, per_device(): lax.psum(partial_value.astype(jnp.bfloat16), 'tp').astype(jnp.float32)  32.9 us
    unnamed x48, local copies, waits for them, and re-layouts  24.7 us
    psum x2, blocking collectives, project_heads(): totals = lax.psum(squares, 'tp')  17.6 us
    gather x1, local copies, waits for them, and re-layouts, per_device(): returned.reshape(expert_count * full_cap, model_width)[flat_slot]  12.4 us
    dot_general x2, matrix products, project_heads(): jnp.dot(normed, weight.reshape(weight.shape[0], 3 * proj_width), preferre...  10.2 us
  transfers between devices with their start and end apart: 4, of which 4 were waited for; matrix products, arithmetic and copies ran while one was open for 7% of the time, Pallas kernels for 0%

commit v1 on v0

v1 whole, which is shorter than its diff:
```python
import functools
import math

import jax
import jax.numpy as jnp
from jax import lax
from jax.experimental import pallas as pl
from jax.experimental.pallas import tpu as pltpu
from jax.sharding import PartitionSpec as P

HD = 128
MESH = pl.DeviceIdType.MESH
F32 = jnp.float32
BF16 = jnp.bfloat16

eps_norm = 1e-05
eps_head = 1e-06
rope_base = 10000.0

ROWS = 128
D = 2048
Q = 32
AUX = 128
DG = D + AUX
NE = 64
CAP = 24
GATHER_PARTS = ((0, 768), (768, 768), (1536, 640))
REDUCE_PARTS = ((0, 768), (768, 640), (1408, 640))
ORDERS = ((1, 2, 0), (2, 0, 1), (0, 1, 2))
VMEM_LIMIT = 60 * 1024 * 1024


def place():
    rep = lax.axis_index("rep")
    return (rep // 8, (rep // 2) % 4, lax.axis_index("tp")), rep % 2


def device(coords, core):
    return (coords[0] * 8 + coords[1] * 2 + core, coords[2])


def moved(coords, axis, step):
    out = list(coords)
    out[axis] = (coords[axis] + step) % 4
    return tuple(out)


def greet(coords, core):
    barrier = pltpu.get_barrier_semaphore()
    peers = [device(coords, 1 - core), device(moved(coords, 2, 2), core)]
    for axis in range(3):
        for step in (1, 3):
            peers.append(device(moved(coords, axis, step), core))
    for peer in peers:
        pl.semaphore_signal(barrier, inc=1, device_id=peer, device_id_type=MESH)
    pl.semaphore_wait(barrier, len(peers))


def window(coords, axes, axis=None, value=None, rows=(0, Q), cols=(0, D)):
    index = []
    for a in range(3):
        if a in axes:
            index.append(pl.ds(0, 4))
        elif a == axis:
            index.append(value)
        else:
            index.append(coords[a])
    return tuple(index) + (pl.ds(rows[0], rows[1]), pl.ds(cols[0], cols[1]))


LO, HI, ALL = (0, 16), (16, 16), (0, Q)


def gather_kernel(part_ref, hidden_ref, gain_ref, aux_ref, g_ref, mid_ref,
                  inbox, own, tp_send, tp_recv, send, recv, sib_send, sib_recv, local_sem):
    coords, core = place()
    y = coords[2]
    greet(coords, core)
    tp_copies = []
    for k in range(1, 4):
        peer = (y + k) % 4
        copy = pltpu.make_async_remote_copy(
            src_ref=part_ref.at[pl.ds(pl.multiple_of(peer * Q, Q), Q), :],
            dst_ref=inbox.at[k - 1],
            send_sem=tp_send.at[k - 1],
            recv_sem=tp_recv.at[k - 1],
            device_id=device(moved(coords, 2, k), core),
            device_id_type=MESH,
        )
        copy.start()
        tp_copies.append(copy)
    rows = pl.ds(pl.multiple_of(y * Q, Q), Q)
    total = part_ref[rows, :].astype(F32)
    for k in range(3):
        tp_copies[k].wait_recv()
    for k in range(3):
        total = total + inbox[k].astype(F32)
    mid = (hidden_ref[rows, :].astype(F32) + total).astype(BF16)
    mid_ref[...] = mid
    wide = mid.astype(F32)
    scale = lax.rsqrt(jnp.mean(wide * wide, axis=-1, keepdims=True) + eps_norm)
    own[:, pl.ds(0, D)] = (wide * scale * gain_ref[...]).astype(BF16)
    own[:, pl.ds(D, AUX)] = aux_ref[rows, :]
    pending = list(tp_copies)
    here = pltpu.make_async_copy(own, g_ref.at[(core,) + coords], local_sem)
    here.start()

    def push(src, index, send_sem, recv_sem, peer):
        copy = pltpu.make_async_remote_copy(
            src_ref=src, dst_ref=g_ref.at[(core,) + index], send_sem=send_sem, recv_sem=recv_sem,
            device_id=peer, device_id_type=MESH,
        )
        copy.start()
        pending.append(copy)
        return copy

    sibling = device(coords, 1 - core)
    arrivals = []

    def forward(index, p, slot):
        arrivals.append(push(g_ref.at[(core,) + index], index, sib_send.at[p, slot], sib_recv.at[p, slot], sibling))

    for phase in range(3):
        steps = []
        for p in range(3):
            axis = ORDERS[p][phase]
            axes = ORDERS[p][:phase]
            cols = GATHER_PARTS[p]
            a = coords[axis]
            index = window(coords, axes, axis, a, ALL, cols)
            src = own.at[:, pl.ds(*cols)] if phase == 0 else g_ref.at[(core,) + index]
            right = device(moved(coords, axis, 1), core)
            left = device(moved(coords, axis, 3), core)
            to_right = push(src, index, send.at[p, phase, 0], recv.at[p, phase, 0], right)
            to_left = push(src, index, send.at[p, phase, 1], recv.at[p, phase, 1], left)
            steps.append((axis, axes, cols, a, right, left, to_right, to_left))
        if phase == 0:
            for p in range(3):
                cols = GATHER_PARTS[p]
                index = window(coords, (), None, None, ALL, cols)
                arrivals.append(push(own.at[:, pl.ds(*cols)], index, sib_send.at[p, 0], sib_recv.at[p, 0], sibling))
        ends = []
        for p in range(3):
            axis, axes, cols, a, right, left, to_right, to_left = steps[p]
            to_right.wait_recv()
            low = window(coords, axes, axis, (a + 3) % 4, LO, cols)
            far_low = push(g_ref.at[(core,) + low], low, send.at[p, phase, 2], recv.at[p, phase, 2], right)
            to_left.wait_recv()
            high = window(coords, axes, axis, (a + 1) % 4, HI, cols)
            far_high = push(g_ref.at[(core,) + high], high, send.at[p, phase, 3], recv.at[p, phase, 3], left)
            forward(window(coords, axes, axis, (a + 3) % 4, ALL, cols), p, 1 + 4 * phase)
            forward(window(coords, axes, axis, (a + 1) % 4, ALL, cols), p, 2 + 4 * phase)
            ends.append((far_low, far_high))
        if phase == 0:
            here.wait()
        for p in range(3):
            axis, axes, cols, a = steps[p][:4]
            ends[p][0].wait_recv()
            forward(window(coords, axes, axis, (a + 2) % 4, LO, cols), p, 3 + 4 * phase)
            ends[p][1].wait_recv()
            forward(window(coords, axes, axis, (a + 2) % 4, HI, cols), p, 4 + 4 * phase)
    for copy in arrivals:
        copy.wait_recv()
    for copy in pending:
        copy.wait_send()


def gather_rows(part, hidden, gain, aux):
    return pl.pallas_call(
        gather_kernel,
        name="dispatch_rows",
        out_shape=(
            jax.ShapeDtypeStruct((2, 4, 4, 4, Q, DG), BF16),
            jax.ShapeDtypeStruct((Q, D), BF16),
        ),
        in_specs=[pl.BlockSpec(memory_space=pltpu.VMEM)] * 4,
        out_specs=(pl.BlockSpec(memory_space=pltpu.HBM), pl.BlockSpec(memory_space=pltpu.VMEM)),
        scratch_shapes=[
            pltpu.VMEM((3, Q, D), BF16),
            pltpu.VMEM((Q, DG), BF16),
            pltpu.SemaphoreType.DMA((3,)),
            pltpu.SemaphoreType.DMA((3,)),
            pltpu.SemaphoreType.DMA((3, 3, 4)),
            pltpu.SemaphoreType.DMA((3, 3, 4)),
            pltpu.SemaphoreType.DMA((3, 13)),
            pltpu.SemaphoreType.DMA((3, 13)),
            pltpu.SemaphoreType.DMA,
        ],
        compiler_params=pltpu.CompilerParams(
            collective_id=0, has_side_effects=True, vmem_limit_bytes=VMEM_LIMIT
        ),
    )(part, hidden, gain, aux)


def expert_kernel(g_ref, gu_ref, down_ref, p_ref, xs, ys, hot, scale):
    rep = lax.axis_index("rep")
    groups = g_ref.shape[0] // 256
    width = 2 * CAP
    lane = lax.broadcasted_iota(jnp.int32, (256, 128), 1)
    row = lax.broadcasted_iota(jnp.int32, (256, 1), 0)
    second = (row >= ROWS).astype(jnp.int32)
    tri_r = lax.broadcasted_iota(jnp.int32, (256, 256), 0)
    tri_c = lax.broadcasted_iota(jnp.int32, (256, 256), 1)
    earlier = jnp.where((tri_c < tri_r) & ((tri_c >= ROWS) == (tri_r >= ROWS)), 1.0, 0.0).astype(BF16)
    slot_lane = lax.broadcasted_iota(jnp.int32, (width, 128), 1)

    def collect(i, carry):
        rows = pl.ds(pl.multiple_of(i * 256, 256), 256)
        weights = g_ref[rows, pl.ds(D, AUX)].astype(F32)
        chosen = jnp.where(weights > 0, 1.0, 0.0)
        ranks = jnp.dot(earlier, chosen.astype(BF16), preferred_element_type=F32)
        match = jnp.zeros((256, 128), F32)
        for j in range(2):
            mine = lane == 2 * rep + j
            picked = jnp.sum(jnp.where(mine, chosen, 0.0), axis=1, keepdims=True)
            rank = jnp.sum(jnp.where(mine, ranks, 0.0), axis=1, keepdims=True).astype(jnp.int32)
            slot = jnp.where(picked > 0, rank + second * CAP + j * width, -1)
            match = match + jnp.where(lane == slot, 1.0, 0.0)
        hot[rows, :] = match.astype(BF16)
        select = match.T.astype(BF16)
        got = jnp.dot(select, g_ref[rows, :], preferred_element_type=F32)
        for j in range(2):
            out_rows = pl.ds(pl.multiple_of(i * width, 16), width)
            block = got[j * width:(j + 1) * width]
            xs[j, out_rows, :] = block[:, :D].astype(BF16)
            wide = block[:, D:]
            mine = (slot_lane == 2 * rep + j) | (slot_lane == 2 * rep + j + NE)
            scale[j, out_rows, :] = jnp.broadcast_to(
                jnp.sum(jnp.where(mine, wide, 0.0), axis=1, keepdims=True), (width, 128))
        return carry

    lax.fori_loop(0, groups, collect, 0)
    for j in range(2):
        x = xs[j]
        gate = jnp.dot(x, gu_ref[j, 0], preferred_element_type=F32)
        up = jnp.dot(x, gu_ref[j, 1], preferred_element_type=F32)
        act = gate / (1.0 + jnp.exp(-gate)) * up
        act = (act * scale[j][:, :1]).astype(BF16)
        ys[j] = jnp.dot(act, down_ref[j], preferred_element_type=F32).astype(BF16)

    def spread(i, carry):
        rows = pl.ds(pl.multiple_of(i * 256, 256), 256)
        in_rows = pl.ds(pl.multiple_of(i * width, 16), width)
        both = jnp.concatenate([ys[0, in_rows, :], ys[1, in_rows, :]], axis=0)
        p_ref[rows, :] = jnp.dot(
            hot[rows, pl.ds(0, 128)][:, :2 * width], both, preferred_element_type=F32).astype(BF16)
        return carry

    lax.fori_loop(0, groups, spread, 0)


def expert_rows(g, gate_up, down):
    step = 1024
    slots = step // 256 * 2 * CAP
    return pl.pallas_call(
        expert_kernel,
        name="experts",
        grid=(g.shape[0] // step,),
        out_shape=jax.ShapeDtypeStruct((g.shape[0], D), BF16),
        in_specs=[
            pl.BlockSpec((step, DG), lambda i: (i, 0)),
            pl.BlockSpec(memory_space=pltpu.VMEM),
            pl.BlockSpec(memory_space=pltpu.VMEM),
        ],
        out_specs=pl.BlockSpec((step, D), lambda i: (i, 0)),
        scratch_shapes=[
            pltpu.VMEM((2, slots, D), BF16),
            pltpu.VMEM((2, slots, D), BF16),
            pltpu.VMEM((step, 128), BF16),
            pltpu.VMEM((2, slots, 128), F32),
        ],
        compiler_params=pltpu.CompilerParams(vmem_limit_bytes=VMEM_LIMIT),
    )(g, gate_up, down)


def reduce_kernel(p_ref, mid_ref, hidden_ref,
                  q, sib, f0, f1, f2, h0, h1, h2, out,
                  load_sem, sib_send, sib_recv, send, recv, tp_send, tp_recv):
    coords, core = place()
    y = coords[2]
    greet(coords, core)
    sibling = device(coords, 1 - core)
    fulls, halves = (f0, f1, f2), (h0, h1, h2)
    loads, exchanges, pending = {}, {}, []
    for n in range(4):
        for p in range(3):
            axis = ORDERS[p][2]
            axes = ORDERS[p][:2]
            value = (coords[axis] + (2, 1, 3, 0)[n]) % 4
            index = window(coords, axes, axis, value, ALL, REDUCE_PARTS[p])
            copy = pltpu.make_async_remote_copy(
                src_ref=p_ref.at[(1 - core,) + index], dst_ref=sib.at[index],
                send_sem=sib_send.at[p, n], recv_sem=sib_recv.at[p, n],
                device_id=sibling, device_id_type=MESH)
            copy.start()
            exchanges[p, n] = copy
            pending.append(copy)
            load = pltpu.make_async_copy(p_ref.at[(core,) + index], q.at[index], load_sem.at[p, n])
            load.start()
            loads[p, n] = load

    def sweep(phase, p, axis, value, body):
        axes = ORDERS[p][:2 - phase]
        free = sorted(axes)

        def one(i):
            inner = (i // 4, i % 4) if len(free) == 2 else ((i,) if len(free) == 1 else ())
            at = [coords[a] for a in range(3)]
            at[axis] = value
            for a, v in zip(free, inner):
                at[a] = v
            body(tuple(at), inner)

        count = 4 ** len(free)
        if count == 1:
            one(0)
        else:
            def step(i, carry):
                one(i)
                return carry
            lax.fori_loop(0, count, step, 0)

    def add_sibling(p, n):
        axis = ORDERS[p][2]
        cols = REDUCE_PARTS[p]
        value = (coords[axis] + (2, 1, 3, 0)[n]) % 4
        loads[p, n].wait()
        exchanges[p, n].wait_recv()

        def body(at, inner):
            spot = at + (slice(None), pl.ds(*cols))
            q[spot] = q[spot] + sib[spot]
        sweep(0, p, axis, value, body)

    def push(phase, p, slot, src_index, dst, peer):
        copy = pltpu.make_async_remote_copy(
            src_ref=q.at[src_index], dst_ref=dst,
            send_sem=send.at[p, phase, slot], recv_sem=recv.at[p, phase, slot],
            device_id=peer, device_id_type=MESH)
        copy.start()
        pending.append(copy)
        return copy

    def band(ref, p, side, axes, rows):
        width = REDUCE_PARTS[p][1]
        lead = (p, side) + (slice(None),) * len(axes)
        return ref.at[lead + (pl.ds(*rows), pl.ds(0, width))]

    for phase in range(3):
        state = []
        for p in range(3):
            axis = ORDERS[p][2 - phase]
            axes = ORDERS[p][:2 - phase]
            cols = REDUCE_PARTS[p]
            a = coords[axis]
            right = device(moved(coords, axis, 1), core)
            left = device(moved(coords, axis, 3), core)
            full, half = fulls[phase], halves[phase]
            if phase == 0:
                add_sibling(p, 0)
            opposite = (a + 2) % 4
            first = push(phase, p, 0, window(coords, axes, axis, opposite, LO, cols), band(half, p, 0, axes, LO), right)
            second = push(phase, p, 1, window(coords, axes, axis, opposite, HI, cols), band(half, p, 1, axes, LO), left)
            state.append((axis, axes, cols, a, right, left, full, half, first, second))
        tails = []
        for p in range(3):
            axis, axes, cols, a, right, left, full, half, first, second = state[p]
            if phase == 0:
                add_sibling(p, 1)
            t0 = push(phase, p, 2, window(coords, axes, axis, (a + 1) % 4, HI, cols), band(full, p, 0, axes, HI), right)
            if phase == 0:
                add_sibling(p, 2)
            t1 = push(phase, p, 3, window(coords, axes, axis, (a + 3) % 4, LO, cols), band(full, p, 1, axes, LO), left)
            tails.append([t0, t1])
        for p in range(3):
            axis, axes, cols, a, right, left, full, half, first, second = state[p]
            for side, came, value, rows, peer, slot in (
                (0, first, (a + 1) % 4, LO, right, 4), (1, second, (a + 3) % 4, HI, left, 5),
            ):
                came.wait_recv()

                def body(at, inner, side=side, rows=rows):
                    spot = at + (pl.ds(*rows), pl.ds(*cols))
                    q[spot] = q[spot] + half[(p, side) + inner + (slice(None), pl.ds(0, cols[1]))]
                sweep(phase, p, axis, value, body)
                tails[p].append(push(phase, p, slot, window(coords, axes, axis, value, rows, cols),
                                     band(full, p, side, axes, rows), peer))
        for p in range(3):
            axis, axes, cols, a, right, left, full, half, first, second = state[p]
            if phase == 0:
                add_sibling(p, 3)
            for copy in tails[p]:
                copy.wait_recv()

            def body(at, inner):
                spot = at + (slice(None), pl.ds(*cols))
                one = full[(p, 0) + inner + (slice(None), pl.ds(0, cols[1]))].astype(F32)
                two = full[(p, 1) + inner + (slice(None), pl.ds(0, cols[1]))].astype(F32)
                total = q[spot].astype(F32) + one + two
                if phase == 2:
                    out[y, :, pl.ds(*cols)] = (mid_ref[:, pl.ds(*cols)].astype(F32) + total).astype(BF16)
                else:
                    q[spot] = total.astype(BF16)
            sweep(phase, p, axis, a, body)
    last = []
    for k in range(1, 4):
        copy = pltpu.make_async_remote_copy(
            src_ref=out.at[y], dst_ref=out.at[y], send_sem=tp_send.at[k - 1], recv_sem=tp_recv.at[k - 1],
            device_id=device(moved(coords, 2, k), core), device_id_type=MESH)
        copy.start()
        last.append(copy)
    for copy in last:
        copy.wait()
    for copy in pending:
        copy.wait_send()
    for b in range(4):
        hidden_ref[pl.ds(b * Q, Q), :] = out[b]


def reduce_rows(partial, mid):
    width = max(w for _, w in REDUCE_PARTS)
    return pl.pallas_call(
        reduce_kernel,
        name="combine_rows",
        out_shape=jax.ShapeDtypeStruct((ROWS, D), BF16),
        in_specs=[pl.BlockSpec(memory_space=pltpu.HBM), pl.BlockSpec(memory_space=pltpu.VMEM)],
        out_specs=pl.BlockSpec(memory_space=pltpu.VMEM),
        scratch_shapes=[
            pltpu.VMEM((4, 4, 4, Q, D), BF16),
            pltpu.VMEM((4, 4, 4, Q, D), BF16),
            pltpu.VMEM((3, 2, 4, 4, Q, width), BF16),
            pltpu.VMEM((3, 2, 4, Q, width), BF16),
            pltpu.VMEM((3, 2, Q, width), BF16),
            pltpu.VMEM((3, 2, 4, 4, Q // 2, width), BF16),
            pltpu.VMEM((3, 2, 4, Q // 2, width), BF16),
            pltpu.VMEM((3, 2, Q // 2, width), BF16),
            pltpu.VMEM((4, Q, D), BF16),
            pltpu.SemaphoreType.DMA((3, 4)),
            pltpu.SemaphoreType.DMA((3, 4)),
            pltpu.SemaphoreType.DMA((3, 4)),
            pltpu.SemaphoreType.DMA((3, 3, 6)),
            pltpu.SemaphoreType.DMA((3, 3, 6)),
            pltpu.SemaphoreType.DMA((3,)),
            pltpu.SemaphoreType.DMA((3,)),
        ],
        compiler_params=pltpu.CompilerParams(
            collective_id=1, has_side_effects=True, vmem_limit_bytes=VMEM_LIMIT
        ),
    )(partial, mid)


def rms_scale(inputs, gain):
    inputs = inputs.astype(F32)
    scaled = inputs * lax.rsqrt(jnp.mean(inputs * inputs, axis=-1, keepdims=True) + eps_norm)
    return (scaled * gain).astype(BF16)


def request_tables(new_lengths, prefix_lengths, row_count, cache_count):
    new_end = jnp.cumsum(new_lengths, dtype=jnp.int32)
    cache_end = jnp.cumsum(prefix_lengths, dtype=jnp.int32)
    token_index = jnp.arange(row_count, dtype=jnp.int32)
    cache_index = jnp.arange(cache_count, dtype=jnp.int32)
    token_request = jnp.sum(
        (token_index[:, None] >= new_end[None, :]).astype(jnp.int32), axis=1, dtype=jnp.int32
    )
    cache_request = jnp.sum(
        (cache_index[:, None] >= cache_end[None, :]).astype(jnp.int32), axis=1, dtype=jnp.int32
    )
    requests = new_lengths.shape[0]
    selector = token_request[:, None] == jnp.arange(requests, dtype=jnp.int32)[None, :]
    new_start = new_end - new_lengths
    offset = token_index - jnp.sum(
        jnp.where(selector, new_start[None, :], 0), axis=1, dtype=jnp.int32
    )
    position = offset + jnp.sum(
        jnp.where(selector, prefix_lengths[None, :], 0), axis=1, dtype=jnp.int32
    )
    return (token_request, cache_request, position)


def project_heads(normed, weight, gains, position, head_size):
    row_count = normed.shape[0]
    proj_width = weight.shape[2]
    full_width = proj_width * lax.axis_size("tp")
    by_member = jnp.transpose(weight, (1, 0, 2))
    projected = [
        jnp.dot(normed, by_member[m], preferred_element_type=F32) for m in range(3)
    ]
    squares = jnp.stack([jnp.sum(projected[m] * projected[m], axis=1) for m in range(2)], axis=1)
    totals = lax.psum(squares, "tp")
    inverse = lax.rsqrt(totals / full_width + eps_head)
    head_count = proj_width // head_size
    half_size = head_size // 2
    frequency = rope_base ** (-jnp.arange(half_size, dtype=F32) * 2.0 / head_size)
    angles = position.astype(F32)[:, None] * frequency[None, :]
    cosine = jnp.cos(angles)[:, None, :]
    sine_table = jnp.sin(angles)[:, None, :]
    outputs = []
    for member in range(2):
        member_rows = projected[member] * inverse[:, member : member + 1]
        portion = (member_rows * gains[member][None, :]).reshape(row_count, head_count, head_size)
        lower_half = portion[..., :half_size]
        upper_half = portion[..., half_size:]
        turned = jnp.concatenate(
            [
                lower_half * cosine - upper_half * sine_table,
                upper_half * cosine + lower_half * sine_table,
            ],
            axis=-1,
        )
        outputs.append(turned.reshape(row_count, proj_width).astype(BF16))
    outputs.append(projected[2].astype(BF16))
    return outputs


def attend(qkv, key_cache, value_cache, token_request, cache_request, head_size):
    row_count, proj_width = qkv[0].shape
    head_count = proj_width // head_size
    queries = qkv[0].reshape(row_count, head_count, head_size)
    key_rows = jnp.concatenate([key_cache, qkv[1]], axis=0).reshape(-1, head_count, head_size)
    value_rows = jnp.concatenate([value_cache, qkv[2]], axis=0).reshape(
        -1, head_count, head_size
    )
    scores = jnp.einsum(
        "qhd,khd->hqk", queries, key_rows, preferred_element_type=F32
    ) / math.sqrt(head_size)
    token_index = jnp.arange(row_count, dtype=jnp.int32)
    cache_ok = cache_request[None, :] == token_request[:, None]
    new_ok = (token_request[None, :] == token_request[:, None]) & (
        token_index[None, :] <= token_index[:, None]
    )
    allowed = jnp.concatenate([cache_ok, new_ok], axis=1)
    scores = jnp.where(allowed[None], scores, -1e30)
    row_max = jnp.max(scores, axis=-1, keepdims=True)
    weights = jnp.exp(scores - row_max)
    weights = (weights / jnp.sum(weights, axis=-1, keepdims=True)).astype(BF16)
    context = jnp.einsum("hqk,khd->qhd", weights, value_rows, preferred_element_type=F32)
    return context.reshape(row_count, proj_width).astype(BF16)


def weight_columns(expert_ids, expert_weights):
    experts = jnp.arange(NE, dtype=jnp.int32)[None, :]
    dense = jnp.zeros((expert_ids.shape[0], NE), F32)
    for k in range(expert_ids.shape[1]):
        dense = dense + jnp.where(expert_ids[:, k:k + 1] == experts, expert_weights[:, k:k + 1], 0.0)
    high = lax.reduce_precision(dense, 8, 7)
    return jnp.concatenate([high, dense - high], axis=1).astype(BF16)


def per_device(
    hidden_in,
    new_lengths,
    prefix_lengths,
    cache_keys,
    cache_values,
    attn_gain,
    w_qkv,
    norm_gains,
    w_out,
    moe_gain,
    expert_ids,
    expert_weights,
    w_gate_up,
    w_down,
    next_gain,
    next_qkv,
    next_norm_gains,
):
    row_count, model_width = hidden_in.shape
    cache_count = cache_keys.shape[0]
    token_request, cache_request, position = request_tables(
        new_lengths[0], prefix_lengths[0], row_count, cache_count
    )
    normed = rms_scale(hidden_in, attn_gain)
    qkv = project_heads(normed, w_qkv, norm_gains, position, HD)
    context = attend(qkv, cache_keys, cache_values, token_request, cache_request, HD)
    attn_part = jnp.dot(context, w_out, preferred_element_type=F32).astype(BF16)
    aux = weight_columns(expert_ids, expert_weights)
    gathered, mid = gather_rows(attn_part, hidden_in, moe_gain[None, :], aux)
    partial = expert_rows(
        gathered.reshape(-1, DG), jnp.transpose(w_gate_up, (0, 2, 1, 3)), w_down)
    hidden_out = reduce_rows(partial.reshape(2, 4, 4, 4, Q, D), mid)
    next_input = rms_scale(hidden_out, next_gain)
    next_out = project_heads(next_input, next_qkv, next_norm_gains, position, HD)
    return (hidden_out, jnp.stack(next_out, axis=1))


def solution(mesh):
    placed = (
        P("rep", None),
        P("rep", None),
        P("rep", None),
        P("rep", "tp"),
        P("rep", "tp"),
        P(),
        P(None, None, "tp"),
        P(None, "tp"),
        P("tp", None),
        P(),
        P("rep", None),
        P("rep", None),
        P("rep", None, None, "tp"),
        P("rep", "tp", None),
        P(),
        P(None, None, "tp"),
        P(None, "tp"),
    )
    return jax.shard_map(
        per_device,
        mesh=mesh,
        in_specs=placed,
        out_specs=(P("rep", None), P("rep", None, "tp")),
        check_vma=False,
    )
```

time: 374 us -> 219 us (0.59)
  the two profiles are of different devices: /device:TPU:1 before, /device:TPU:0 now
where the time goes in v1:
time: 219 us; the launch traced here: 218 us
  Pallas kernels  158 us (72%)
  matrix products  21.1 us (10%)
  blocking collectives  19.1 us (9%)
  local copies, waits for them, and re-layouts  10.7 us (5%)
  other arithmetic  8.54 us (4%)
    pallas_call x1, Pallas kernels, gather_rows(): pl.pallas_call(gather_kernel, name='dispatch_rows', out_shape=(jax.ShapeD...  64.8 us
    pallas_call x1, Pallas kernels, reduce_rows(): pl.pallas_call(reduce_kernel, name='combine_rows', out_shape=jax.ShapeDty...  62.1 us
    pallas_call x1, Pallas kernels, expert_rows(): pl.pallas_call(expert_kernel, name='experts', grid=(g.shape[0] // step,),...  31 us
    psum x2, blocking collectives, project_heads(): totals = lax.psum(squares, 'tp')  19.1 us
    dot_general x6, matrix products, project_heads(): jnp.dot(normed, by_member[m], preferred_element_type=F32)  13.4 us
    unnamed x41, local copies, waits for them, and re-layouts  7.74 us

profile of v1, /device:TPU:0, one launch (start us, length us, event | category | flops | bytes accessed | tf_op | source)
XLA Modules:
  0.0 218.5 jit_solution(1017283255549828364)
XLA Ops:
  0.6 0.0 copy-start
  0.6 0.0 copy-start.3
  0.7 1.4 fusion.15
  2.1 2.3 %multiply_reduce_fusion.2 = (f32[128]{0:T(128)S(1)}, f32[128,512]{1,0:T(8,128)S(1)}) fusion(bf16[3,2048,512]{2,1,0:T(8,128)(2,1)} %bitcast.138, bf16[128,2048]{1,0:T(8,128)(2,1)} %hidden_ref.1, f32[2048]{0:T(1024)} %param.22, f32[128]{0:T(128)S(1)} %add_rsqrt_fusion.3), kind=kOutput, calls=%fused_computation.53 | convolution fusion | flops 269614976 | bytes 2892800 | tf_op jit(solution)/shard_map/dot_general | solution.py:487
  4.4 0.0 copy-start.7
  4.4 2.2 multiply_reduce_fusion.3
  6.6 0.0 copy-start.14
  6.6 0.0 copy-start.11
  6.7 10.8 %psum.14 = f32[128,2]{0,1:T(2,128)S(1)} all-reduce(f32[128,2]{0,1:T(2,128)S(1)} %pad_maximum_fusion.7), channel_id=1, replica_groups=mesh['rep'=32,'tp'=4] {'tp'}, use_global_device_ids=true, to_apply=%region_7.8 | all-reduce | flops 256 | bytes 2048 | tf_op jit(solution)/shard_map/psum | solution.py:490
  17.5 0.1 multiply_multiply_fusion.2
  17.6 0.1 reshape.183
  17.7 0.2 fusion.45
  17.9 0.1 reshape.185
  18.0 0.2 fusion.46
  18.2 0.2 reduce-window.14
  18.4 0.1 convert_reduce_fusion.1
  18.5 0.1 select_reduce_fusion.1
  18.6 0.3 multiply_cosine_fusion
  18.9 0.8 subtract_convert_fusion.3
  19.8 0.1 pad_maximum_fusion.3
  19.9 0.1 copy.49
  20.0 0.0 copy-start.6
  20.0 1.5 copy.50
  21.6 1.1 pad_maximum_fusion.1
  22.7 0.2 reduce-window.13
  22.9 0.1 convert_reduce_fusion
  23.0 0.1 broadcast_compare_fusion
  23.1 0.1 fusion.27
  23.2 0.0 copy-start.4
  23.2 3.8 %fusion.49 = (f32[4,128]{1,0:T(4,128)S(1)}, f32[4,128,1152]{2,1,0:T(8,128)}) fusion(bf16[1152,4,128]{0,2,1:T(8,128)(2,1)} %bitcast.118, pred[128,1152]{1,0:T(8,128)(4,1)S(1)} %pad_add_fusion, bf16[128,4,64]{2,0,1:T(8,128)(2,1)} %get-tuple-element.13, bf16[128,4,64]{2,0,1:T(8,128)(2,1)S(1)} %copy-done.6), kind=kOutput, calls=%fused_computation.127 | convolution fusion | flops 153617536 | bytes 3819520 | tf_op jit(solution)/shard_map/sub | solution.py:535
  27.1 2.2 fusion.11
  29.3 0.1 pad_maximum_fusion
  29.3 1.4 copy.44
  30.8 2.6 %fusion.13 = bf16[4,128,128]{2,1,0:T(8,128)(2,1)S(1)} fusion(bf16[1152,4,128]{0,2,1:T(8,128)(2,1)} %bitcast.119, f32[4,128,1152]{2,1,0:T(8,128)} %get-tuple-element.61, f32[4,128]{1,0:T(4,128)S(1)} %get-tuple-element.60), kind=kOutput, calls=%fused_computation.29 | convolution fusion | flops 152240128 | bytes 3672064 | tf_op jit(solution)/shard_map/hqk,khd->qhd/dot_general | solution.py:537
  33.4 0.0 copy-start.8
  33.4 1.3 convolution_convert_fusion.part_ref
  34.7 0.3 reduce-precision_convert_fusion
  35.1 0.7 pad_maximum_fusion.6.aux_ref
  35.8 64.8 %dispatch_rows.1 = (bf16[2,4,4,4,32,2176]{5,4,3,2,1,0:T(8,128)(2,1)}, bf16[32,2048]{1,0:T(8,128)(2,1)}) custom-call(bf16[128,2048]{1,0:T(8,128)(2,1)} %convolution_convert_fusion.part_ref, bf16[128,2048]{1,0:T(8,128)(2,1)} %hidden_ref.1, f32[1,2048]{1,0:T(1,128)} %bitcast.126, bf16[128,128]{1,0:T(8,128)(2,1)} %pad_maximum_fusion.6.aux_ref), custom_call_target="tpu_custom_call" | custom-call | tf_op jit(solution)/shard_map/dispatch_rows/pallas_call | solution.py:169
  100.6 4.8 %copy.81 = bf16[2,2048,2,256]{3,1,2,0:T(8,128)(2,1)} copy(bf16[2,2048,2,256]{3,2,1,0:T(2,128)(2,1)} %param.29) | data formatting | bytes 8388608 | tf_op args[12]
  105.4 31.0 %experts.1 = bf16[4096,2048]{1,0:T(8,128)(2,1)} custom-call(bf16[4096,2176]{1,0:T(8,128)(2,1)} %bitcast.116, bf16[2,2,2048,256]{3,2,1,0:T(8,128)(2,1)} %bitcast.117, bf16[2,256,2048]{2,1,0:T(8,128)(2,1)} %down_ref.1), custom_call_target="tpu_custom_call" | custom-call | tf_op jit(solution)/shard_map/experts/pallas_call | solution.py:255
  136.4 62.1 %combine_rows.1 = bf16[128,2048]{1,0:T(8,128)(2,1)} custom-call(bf16[2,4,4,4,32,2048]{5,4,3,2,1,0:T(8,128)(2,1)} %bitcast.115, bf16[32,2048]{1,0:T(8,128)(2,1)} %get-tuple-element.5.mid_ref), custom_call_target="tpu_custom_call" | custom-call | tf_op jit(solution)/shard_map/combine_rows/pallas_call | solution.py:422
  198.6 1.3 fusion.18
  199.9 2.3 %multiply_reduce_fusion = (f32[128]{0:T(128)S(1)}, f32[128,512]{1,0:T(8,128)S(1)}) fusion(bf16[3,2048,512]{2,1,0:T(8,128)(2,1)} %bitcast.141, bf16[128,2048]{1,0:T(8,128)(2,1)} %combine_rows.1, f32[2048]{0:T(1024)S(1)} %copy-done.13, f32[128]{0:T(128)S(1)} %add_rsqrt_fusion.2), kind=kOutput, calls=%fused_computation.45 | convolution fusion | flops 269614976 | bytes 2892800 | tf_op jit(solution)/shard_map/dot_general | solution.py:487
  202.3 2.2 multiply_reduce_fusion.1
  204.4 8.3 %psum.15 = f32[128,2]{0,1:T(2,128)S(1)} all-reduce(f32[128,2]{0,1:T(2,128)S(1)} %pad_maximum_fusion.8), channel_id=1, replica_groups=mesh['rep'=32,'tp'=4] {'tp'}, use_global_device_ids=true, to_apply=%region_15.16 | all-reduce | flops 256 | bytes 2048 | tf_op jit(solution)/shard_map/psum | solution.py:490
  212.7 0.1 multiply_multiply_fusion
  212.8 0.1 copy.57
  213.0 0.1 copy.70
  213.1 0.1 copy.71
  213.2 0.1 multiply_multiply_fusion.1
  213.3 0.1 copy.53
  213.5 0.1 copy.68
  213.6 0.1 copy.69
  213.8 0.1 subtract_convert_fusion.1
  213.9 0.1 pad_maximum_fusion.4
  214.0 0.1 copy.56
  214.2 0.1 copy.61
  214.3 0.1 pad_maximum_fusion.5
  214.4 0.1 copy.60
  214.6 0.1 copy.62
  214.7 2.2 %fusion.14 = bf16[128,1,512]{2,0,1:T(8,128)(2,1)S(1)} fusion(bf16[3,2048,512]{2,1,0:T(8,128)(2,1)} %bitcast.143, bf16[128,2048]{1,0:T(8,128)(2,1)S(1)} %copy-done.2, f32[2048]{0:T(1024)S(1)} %copy-done.13, f32[128]{0:T(128)S(1)} %add_rsqrt_fusion.2), kind=kOutput, calls=%fused_computation.30 | convolution fusion | flops 269549568 | bytes 2761216 | tf_op jit(solution)/shard_map/dot_general | solution.py:487
  216.9 0.8 pad_maximum_fusion.2
  217.7 0.8 copy.83
  (44 shorter events, 0.2 us)
Async XLA Ops:
  0.6 32.8 %copy-start = (bf16[512,2048]{1,0:T(8,128)(2,1)S(1)}, bf16[512,2048]{1,0:T(8,128)(2,1)}, u32[]{:S(2)}) copy-start(bf16[512,2048]{1,0:T(8,128)(2,1)} %param.25) | copy-start | bytes 6291460
  0.6 3.8 %copy-start.3 = (bf16[128,2048]{1,0:T(8,128)(2,1)S(1)}, bf16[128,2048]{1,0:T(8,128)(2,1)}, u32[]{:S(2)}) copy-start(bf16[128,2048]{1,0:T(8,128)(2,1)} %hidden_ref.1) | copy-start | bytes 1572868
  0.7 3.8 %copy-start.12 = (f32[2048]{0:T(1024)S(1)}, f32[2048]{0:T(1024)}, u32[]{:S(2)}) copy-start(f32[2048]{0:T(1024)} %param.22) | copy-start | bytes 24580
  2.1 4.5 %copy-start.15 = (f32[128]{0:T(128)}, f32[128]{0:T(128)S(1)}, u32[]{:S(2)}) copy-start(f32[128]{0:T(128)S(1)} %add_rsqrt_fusion.3) | copy-start | bytes 1540
  4.4 13.1 %copy-start.7 = (f32[2,512]{1,0:T(2,128)S(1)}, f32[2,512]{1,0:T(2,128)}, u32[]{:S(2)}) copy-start(f32[2,512]{1,0:T(2,128)} %param.24) | copy-start | bytes 12292
  6.6 11.6 %copy-start.14 = (s32[1,4]{1,0:T(1,128)S(1)}, s32[1,4]{1,0:T(1,128)}, u32[]{:S(2)}) copy-start(s32[1,4]{1,0:T(1,128)} %param.18) | copy-start | bytes 52
  6.6 11.9 %copy-start.11 = (s32[1,4]{1,0:T(1,128)S(1)}, s32[1,4]{1,0:T(1,128)}, u32[]{:S(2)}) copy-start(s32[1,4]{1,0:T(1,128)} %param.19) | copy-start | bytes 52
  20.0 3.2 %copy-start.6 = (bf16[128,4,64]{2,0,1:T(8,128)(2,1)S(1)}, bf16[128,4,64]{2,0,1:T(8,128)(2,1)}, u32[]{:S(2)}) copy-start(bf16[128,4,64]{2,0,1:T(8,128)(2,1)} %get-tuple-element.12) | copy-start | bytes 196612
  23.2 3.8 %copy-start.4 = (bf16[128,2048]{1,0:T(8,128)(2,1)S(1)}, bf16[128,2048]{1,0:T(8,128)(2,1)}, u32[]{:S(2)}) copy-start(bf16[128,2048]{1,0:T(8,128)(2,1)} %hidden_ref.1) | copy-start | bytes 1572868
  23.2 3.8 %copy-start.16 = (f32[128]{0:T(128)S(1)}, f32[128]{0:T(128)}, u32[]{:S(2)}) copy-start(f32[128]{0:T(128)} %copy-done.15) | copy-start | bytes 1540
  27.1 2.2 %copy-start.5 = (bf16[1024,512]{1,0:T(8,128)(2,1)S(1)}, bf16[1024,512]{1,0:T(8,128)(2,1)}, u32[]{:S(2)}) copy-start(bf16[1024,512]{1,0:T(8,128)(2,1)} %param.21) | copy-start | bytes 3145732
  33.4 1.3 copy-start.8
  33.4 1.3 copy-start.9
  136.4 63.4 %copy-start.13 = (f32[2048]{0:T(1024)S(1)}, f32[2048]{0:T(1024)}, u32[]{:S(2)}) copy-start(f32[2048]{0:T(1024)} %param.31) | copy-start | bytes 24580
  198.6 3.7 %copy-start.2 = (bf16[128,2048]{1,0:T(8,128)(2,1)S(1)}, bf16[128,2048]{1,0:T(8,128)(2,1)}, u32[]{:S(2)}) copy-start(bf16[128,2048]{1,0:T(8,128)(2,1)} %combine_rows.1) | copy-start | bytes 1572868
  202.2 10.5 %copy-start.10 = (f32[2,512]{1,0:T(2,128)S(1)}, f32[2,512]{1,0:T(2,128)}, u32[]{:S(2)}) copy-start(f32[2,512]{1,0:T(2,128)} %param.33) | copy-start | bytes 12292
  214.5 3.9 %copy-start.1 = (bf16[512,2048]{1,0:T(8,128)(2,1)S(1)}, bf16[512,2048]{1,0:T(8,128)(2,1)}, u32[]{:S(2)}) copy-start(bf16[512,2048]{1,0:T(8,128)(2,1)} %param.25) | copy-start | bytes 6291460

commit v2 on v0

v2 whole, which is shorter than its diff:
```python
import functools
import math

import jax
import jax.numpy as jnp
from jax import lax
from jax.experimental import pallas as pl
from jax.experimental.pallas import tpu as pltpu
from jax.sharding import PartitionSpec as P

HD = 128
MESH = pl.DeviceIdType.MESH
F32 = jnp.float32
BF16 = jnp.bfloat16

eps_norm = 1e-05
eps_head = 1e-06
rope_base = 10000.0

ROWS = 128
D = 2048
Q = 32
AUX = 128
HALF = D // 2
WIDE = HALF + AUX
NE = 64
CAP = 24
GATHER_PARTS = ((0, 384), (384, 384), (768, 384))
REDUCE_PARTS = ((0, 384), (384, 384), (768, 256))
ORDERS = ((1, 2, 0), (2, 0, 1), (0, 1, 2))
VMEM_LIMIT = 60 * 1024 * 1024


def place():
    rep = lax.axis_index("rep")
    return (rep // 8, (rep // 2) % 4, lax.axis_index("tp")), rep % 2


def device(coords, core):
    return (coords[0] * 8 + coords[1] * 2 + core, coords[2])


def moved(coords, axis, step):
    out = list(coords)
    out[axis] = (coords[axis] + step) % 4
    return tuple(out)


def greet(coords, core):
    barrier = pltpu.get_barrier_semaphore()
    peers = [device(coords, 1 - core)]
    for axis in range(3):
        for step in (1, 2, 3):
            peers.append(device(moved(coords, axis, step), core))
    for peer in peers:
        pl.semaphore_signal(barrier, inc=1, device_id=peer, device_id_type=MESH)
    pl.semaphore_wait(barrier, len(peers))


WHOLE = pl.ds(0, 4)
LO, HI, ALL = (0, 16), (16, 16), (0, Q)
WIDTH = 2 * CAP
SLOTS = 16 * CAP


def window(coords, at, rows, cols):
    index = tuple(at.get(axis, coords[axis]) for axis in range(3))
    return index + (pl.ds(*rows), pl.ds(*cols))


def moe_kernel(part_ref, hidden_ref, gain_ref, aux_ref, gu_hbm, down_hbm, out_ref, g_ref,
               inbox, own, mid, gu, down, gbuf, xs, ys, hot, scale, part, sib,
               near, far, mnear, mfar, first, result, other, out,
               tp_send, tp_recv, ag_send, ag_recv, share_send, share_recv, local_sem, load_sem, weight_sem,
               sib_send, sib_recv, rs_send, rs_recv, swap_send, swap_recv, end_send, end_recv):
    coords, core = place()
    rep = lax.axis_index("rep")
    y = coords[2]
    sibling = device(coords, 1 - core)
    pending = []
    fetch = [pltpu.make_async_copy(gu_hbm, gu, weight_sem.at[0]), pltpu.make_async_copy(down_hbm, down, weight_sem.at[1])]
    for copy in fetch:
        copy.start()
    greet(coords, core)

    def push(src, dst, send_sem, recv_sem, peer):
        copy = pltpu.make_async_remote_copy(
            src_ref=src, dst_ref=dst, send_sem=send_sem, recv_sem=recv_sem, device_id=peer, device_id_type=MESH)
        copy.start()
        pending.append(copy)
        return copy

    tp_copies = []
    for k in (2, 1, 3):
        peer = (y + k) % 4
        tp_copies.append(push(
            part_ref.at[pl.ds(pl.multiple_of(peer * Q, Q), Q), :], inbox.at[k - 1],
            tp_send.at[k - 1], tp_recv.at[k - 1], device(moved(coords, 2, k), core)))
    rows = pl.ds(pl.multiple_of(y * Q, Q), Q)
    total = part_ref[rows, :].astype(F32)
    for copy in tp_copies:
        copy.wait_recv()
    for k in range(3):
        total = total + inbox[k].astype(F32)
    stream = (hidden_ref[rows, :].astype(F32) + total).astype(BF16)
    mid[...] = stream
    wide = stream.astype(F32)
    inverse = lax.rsqrt(jnp.mean(wide * wide, axis=-1, keepdims=True) + eps_norm)
    normed = (wide * inverse * gain_ref[...]).astype(BF16)
    for h in range(2):
        own[2 + h, :, pl.ds(0, HALF)] = normed[:, h * HALF:(h + 1) * HALF]
        own[2 + h, :, pl.ds(HALF, AUX)] = aux_ref[rows, :]
    own[core] = own[2 + core]
    swap = push(own.at[2 + (1 - core)], own.at[core], swap_send.at[0], swap_recv.at[0], sibling)
    return_own = swap

    def gather(chunk):
        def at(index):
            return g_ref.at[(chunk, core) + index]

        arrivals = []

        def share(p, slot, index, src=None):
            arrivals.append(push(at(index) if src is None else src, at(index),
                                 share_send.at[chunk, p, slot], share_recv.at[chunk, p, slot], sibling))

        class Ring:
            def __init__(self, p, number, axis, where):
                self.p, self.base, self.axis, self.where = p, number * 4, axis, where
                self.a = coords[axis]
                self.right = device(moved(coords, axis, 1), core)
                self.left = device(moved(coords, axis, 3), core)
                self.ends = [self.push(0, self.index(0), self.right), self.push(1, self.index(0), self.left)]

            def index(self, step, rows=ALL):
                return window(coords, {**self.where, self.axis: (self.a + step) % 4}, rows, GATHER_PARTS[self.p])

            def push(self, k, index, peer):
                n = self.base + k
                return push(at(index), at(index), ag_send.at[chunk, self.p, n], ag_recv.at[chunk, self.p, n], peer)

            def near(self):
                for k, step, rows, peer in ((0, 3, LO, self.right), (1, 1, HI, self.left)):
                    self.ends[k].wait_recv()
                    self.ends.append(self.push(2 + k, self.index(step, rows), peer))

            def far(self):
                self.ends[2].wait_recv()
                self.ends[3].wait_recv()

        firsts = []
        for p in range(3):
            axis = ORDERS[p][0]
            index = window(coords, {}, ALL, GATHER_PARTS[p])
            src = own.at[chunk, :, pl.ds(*GATHER_PARTS[p])]
            firsts.append([
                push(src, at(index), ag_send.at[chunk, p, k - 1], ag_recv.at[chunk, p, k - 1],
                     device(moved(coords, axis, k), core))
                for k in (1, 3, 2)
            ])
        here = pltpu.make_async_copy(own.at[chunk], g_ref.at[(chunk, core) + coords], local_sem.at[chunk])
        here.start()
        yield
        here.wait()
        rings = []
        for p in range(3):
            for copy in firsts[p]:
                copy.wait_recv()
            rings.append(Ring(p, 1, ORDERS[p][1], {ORDERS[p][0]: WHOLE}))
        yield
        for ring in rings:
            ring.near()
        yield
        for p in range(3):
            one, two, three = ORDERS[p]
            rings[p].far()
            rings[p] = Ring(p, 2, three, {one: WHOLE, two: WHOLE})
            share(p, 0, rings[p].index(0))
        yield
        for p in range(3):
            rings[p].near()
            share(p, 1, rings[p].index(3))
            share(p, 2, rings[p].index(1))
        yield
        for p in range(3):
            rings[p].far()
            share(p, 3, rings[p].index(2))
        yield
        for copy in arrivals:
            copy.wait_recv()

    lane = lax.broadcasted_iota(jnp.int32, (256, 128), 1)
    second = (lax.broadcasted_iota(jnp.int32, (256, 1), 0) >= ROWS).astype(jnp.int32)
    slot_lane = lax.broadcasted_iota(jnp.int32, (WIDTH, 128), 1)

    def experts(chunk):
        def load(z):
            copies = [
                pltpu.make_async_copy(g_ref.at[chunk, h, z], gbuf.at[z % 2, h], load_sem.at[z % 2, h]) for h in range(2)
            ]
            for copy in copies:
                copy.start()
            return copies

        def collect(z, i):
            tri_r = lax.broadcasted_iota(jnp.int32, (256, 256), 0)
            tri_c = lax.broadcasted_iota(jnp.int32, (256, 256), 1)
            earlier = jnp.where((tri_c < tri_r) & ((tri_c >= ROWS) == (tri_r >= ROWS)), 1.0, 0.0).astype(BF16)
            blocks = pl.ds(2 * i, 2)
            low = gbuf[z % 2, 0, blocks].reshape(256, WIDE)
            high = gbuf[z % 2, 1, blocks].reshape(256, WIDE)[:, :HALF]
            chosen = jnp.where(low[:, HALF:].astype(F32) > 0, 1.0, 0.0)
            ranks = jnp.dot(earlier, chosen.astype(BF16), preferred_element_type=F32)
            match = jnp.zeros((256, 128), F32)
            for j in range(2):
                mine = lane == 2 * rep + j
                picked = jnp.sum(jnp.where(mine, chosen, 0.0), axis=1, keepdims=True)
                rank = jnp.sum(jnp.where(mine, ranks, 0.0), axis=1, keepdims=True).astype(jnp.int32)
                slot = jnp.where(picked > 0, rank + second * CAP + j * WIDTH, -1)
                match = match + jnp.where(lane == slot, 1.0, 0.0)
            hot[2 * z + i] = match.astype(BF16)
            select = match.T[:2 * WIDTH].astype(BF16)
            got_low = jnp.dot(select, low, preferred_element_type=F32)
            got_high = jnp.dot(select, high, preferred_element_type=F32)
            slots = pl.ds(pl.multiple_of((2 * z + i) * WIDTH, 16), WIDTH)
            for j in range(2):
                span = slice(j * WIDTH, (j + 1) * WIDTH)
                xs[j, slots, pl.ds(0, HALF)] = got_low[span, :HALF].astype(BF16)
                xs[j, slots, pl.ds(HALF, HALF)] = got_high[span].astype(BF16)
                mine = (slot_lane == 2 * rep + j) | (slot_lane == 2 * rep + j + NE)
                scale[j, slots, :] = jnp.broadcast_to(
                    jnp.sum(jnp.where(mine, got_low[span, HALF:], 0.0), axis=1, keepdims=True), (WIDTH, 128))

        def looped(body, z):
            def step(i, carry):
                body(z, i)
                return carry
            lax.fori_loop(0, 2, step, 0)

        def spread(z, i):
            slots = pl.ds(pl.multiple_of((2 * z + i) * WIDTH, 16), WIDTH)
            both = jnp.concatenate([ys[0, slots, :], ys[1, slots, :]], axis=0)
            back = jnp.dot(hot[2 * z + i][:, :2 * WIDTH], both, preferred_element_type=F32).astype(BF16)
            for h in range(2):
                part[chunk, h, z, pl.ds(2 * i, 2)] = back[:, h * HALF:(h + 1) * HALF].reshape(2, 4, Q, HALF)

        copies = load(0)
        for z in range(4):
            coming = load(z + 1) if z < 3 else None
            for copy in copies:
                copy.wait()
            looped(collect, z)
            copies = coming
            yield
        if chunk == 0:
            for copy in fetch:
                copy.wait()
        for j in range(2):
            x = xs[j]
            gate = jnp.dot(x, gu[j, 0], preferred_element_type=F32)
            up = jnp.dot(x, gu[j, 1], preferred_element_type=F32)
            act = gate / (1.0 + jnp.exp(-gate)) * up
            act = (act * scale[j][:, :1]).astype(BF16)
            ys[j] = jnp.dot(act, down[j], preferred_element_type=F32).astype(BF16)
            yield
        for z in range(4):
            looped(spread, z)
            yield

    def reduce(chunk):
        exchanges = {}
        for step in (2, 1, 3, 0):
            for p in range(3):
                one, two, three = ORDERS[p]
                index = window(coords, {one: WHOLE, two: WHOLE, three: (coords[three] + step) % 4}, ALL, REDUCE_PARTS[p])
                exchanges[p, step] = push(part.at[(chunk, 1 - core) + index], sib.at[(chunk,) + index],
                                          sib_send.at[chunk, p, step], sib_recv.at[chunk, p, step], sibling)

        def sweep(where, body):
            free = [axis for axis in range(3) if axis in where and where[axis] is WHOLE]

            def one(i):
                inner = (i // 4, i % 4) if len(free) == 2 else ((i,) if len(free) == 1 else ())
                spot = [where.get(axis, coords[axis]) for axis in range(3)]
                for axis, v in zip(free, inner):
                    spot[axis] = v
                body(tuple(spot), inner)

            if not free:
                one(0)
            else:
                def step(i, carry):
                    one(i)
                    return carry
                lax.fori_loop(0, 4 ** len(free), step, 0)

        class Ring:
            def __init__(self, p, number, axis, where, halves, fulls):
                self.p, self.base, self.axis, self.where = p, number * 6, axis, where
                self.halves, self.fulls = halves, fulls
                self.a = coords[axis]
                self.peers = (device(moved(coords, axis, 1), core), device(moved(coords, axis, 3), core))
                self.free = sum(v is WHOLE for v in where.values())
                self.came, self.tails = [], []

            def blocks(self, step):
                return {**self.where, self.axis: (self.a + step) % 4}

            def push(self, k, step, rows, which, side, lead):
                index = window(coords, self.blocks(step), rows, REDUCE_PARTS[self.p])
                dst = which.at[lead + (slice(None),) * self.free + (pl.ds(*rows), pl.ds(0, REDUCE_PARTS[self.p][1]))]
                n = self.base + k
                return push(part.at[(chunk, core) + index], dst,
                            rs_send.at[chunk, self.p, n], rs_recv.at[chunk, self.p, n], self.peers[side])

            def far(self):
                self.came = [self.push(0, 2, LO, self.halves, 0, ()), self.push(1, 2, HI, self.halves, 1, ())]

            def near(self, side):
                step, rows = ((1, HI), (3, LO))[side]
                self.tails.append(self.push(2 + side, step, rows, self.fulls, side, (side,)))

            def relay(self):
                cols = REDUCE_PARTS[self.p]
                for side, (step, rows) in enumerate(((1, LO), (3, HI))):
                    self.came[side].wait_recv()

                    def body(spot, inner, side=side, rows=rows):
                        spot = (chunk, core) + spot + (pl.ds(*rows), pl.ds(*cols))
                        part[spot] = part[spot] + self.halves[inner + (pl.ds(*rows), pl.ds(0, cols[1]))]
                    sweep(self.blocks(step), body)
                    self.tails.append(self.push(4 + side, step, rows, self.fulls, side, (side,)))

            def finish(self):
                cols = REDUCE_PARTS[self.p]
                for copy in self.tails:
                    copy.wait_recv()

                def body(spot, inner):
                    spot = (chunk, core) + spot + (slice(None), pl.ds(*cols))
                    one = self.fulls[(0,) + inner + (slice(None), pl.ds(0, cols[1]))].astype(F32)
                    two = self.fulls[(1,) + inner + (slice(None), pl.ds(0, cols[1]))].astype(F32)
                    part[spot] = (part[spot].astype(F32) + one + two).astype(BF16)
                sweep(self.blocks(0), body)

        outer, inner = [], []
        for p in range(3):
            one, two, three = ORDERS[p]
            outer.append(Ring(p, 0, three, {one: WHOLE, two: WHOLE}, near.at[chunk, p], far.at[chunk, p]))
            inner.append(Ring(p, 1, two, {one: WHOLE}, mnear.at[chunk, p], mfar.at[chunk, p]))

        def settle(p, step):
            cols = REDUCE_PARTS[p]
            exchanges[p, step].wait_recv()

            def body(spot, _):
                spot = spot + (slice(None), pl.ds(*cols))
                mine = (chunk, core) + spot
                part[mine] = part[mine] + sib[(chunk,) + spot]
            sweep(outer[p].blocks(step), body)

        yield
        for p in range(3):
            settle(p, 2)
            outer[p].far()
        yield
        for p in range(3):
            settle(p, 1)
            outer[p].near(0)
            settle(p, 3)
            outer[p].near(1)
        yield
        for p in range(3):
            outer[p].relay()
        yield
        for p in range(3):
            settle(p, 0)
        yield
        for p in range(3):
            outer[p].finish()
            inner[p].far()
            inner[p].near(0)
            inner[p].near(1)
        yield
        for p in range(3):
            inner[p].relay()
        yield
        ends = []
        for p in range(3):
            inner[p].finish()
            axis = ORDERS[p][0]
            copies = []
            for k in (1, 3, 2):
                index = window(coords, {axis: (coords[axis] + k) % 4}, ALL, REDUCE_PARTS[p])
                dst = first.at[chunk, p, k - 1, :, pl.ds(0, REDUCE_PARTS[p][1])]
                copies.append(push(part.at[(chunk, core) + index], dst, rs_send.at[chunk, p, 11 + k],
                                   rs_recv.at[chunk, p, 11 + k], device(moved(coords, axis, k), core)))
            ends.append(copies)
        yield
        for p in range(3):
            cols = REDUCE_PARTS[p]
            for copy in ends[p]:
                copy.wait_recv()
            total = part[(chunk, core) + coords + (slice(None), pl.ds(*cols))].astype(F32)
            for k in range(3):
                total = total + first[chunk, p, k, :, pl.ds(0, cols[1])].astype(F32)
            result[chunk, :, pl.ds(*cols)] = total.astype(BF16)

    def advance(process, count=1):
        for _ in range(count):
            next(process, None)

    gathers = [gather(0), gather(1)]
    return_own.wait_recv()
    advance(gathers[0])
    advance(gathers[1])
    advance(gathers[0])
    advance(gathers[0])
    advance(gathers[1])
    advance(gathers[0])
    advance(gathers[1])
    advance(gathers[0])
    advance(gathers[1])
    advance(gathers[0], 2)
    work = experts(0)
    advance(work, 8)
    advance(gathers[1])
    advance(work, 99)
    sums = [reduce(0), reduce(1)]
    advance(sums[0])
    advance(gathers[1])
    advance(sums[0], 2)
    advance(gathers[1])
    work = experts(1)
    advance(work, 2)
    advance(sums[0])
    advance(work, 2)
    advance(sums[0])
    advance(work, 1)
    advance(sums[0])
    advance(work, 1)
    advance(sums[0])
    advance(work, 2)
    advance(sums[0])
    advance(work, 99)
    advance(sums[1], 3)
    advance(sums[0], 99)
    advance(sums[1], 99)
    trade = push(result.at[1 - core], other, swap_send.at[1], swap_recv.at[1], sibling)
    trade.wait_recv()
    for h in range(2):
        cols = pl.ds(h * HALF, HALF)
        term = jnp.where(core == h, result[core].astype(F32), other[...].astype(F32))
        out[y, :, cols] = (mid[:, cols].astype(F32) + term).astype(BF16)
    final = [
        push(out.at[y], out.at[y], end_send.at[k - 1], end_recv.at[k - 1], device(moved(coords, 2, k), core))
        for k in (2, 1, 3)
    ]
    for copy in final:
        copy.wait_recv()
    for copy in pending:
        copy.wait_send()
    for b in range(4):
        out_ref[pl.ds(b * Q, Q), :] = out[b]


def moe(part, hidden, gain, aux, gate_up, down):
    wide = max(w for _, w in REDUCE_PARTS)
    dma = pltpu.SemaphoreType.DMA
    return pl.pallas_call(
        moe_kernel,
        name="moe",
        out_shape=(
            jax.ShapeDtypeStruct((ROWS, D), BF16),
            jax.ShapeDtypeStruct((2, 2, 4, 4, 4, Q, WIDE), BF16),
        ),
        in_specs=[pl.BlockSpec(memory_space=pltpu.VMEM)] * 4 + [pl.BlockSpec(memory_space=pltpu.HBM)] * 2,
        out_specs=(pl.BlockSpec(memory_space=pltpu.VMEM), pl.BlockSpec(memory_space=pltpu.HBM)),
        scratch_shapes=[
            pltpu.VMEM((3, Q, D), BF16),
            pltpu.VMEM((4, Q, WIDE), BF16),
            pltpu.VMEM((Q, D), BF16),
            pltpu.VMEM(gate_up.shape, BF16),
            pltpu.VMEM(down.shape, BF16),
            pltpu.VMEM((2, 2, 4, 4, Q, WIDE), BF16),
            pltpu.VMEM((2, SLOTS, D), BF16),
            pltpu.VMEM((2, SLOTS, D), BF16),
            pltpu.VMEM((8, 256, 128), BF16),
            pltpu.VMEM((2, SLOTS, 128), F32),
            pltpu.VMEM((2, 2, 4, 4, 4, Q, HALF), BF16),
            pltpu.VMEM((2, 4, 4, 4, Q, HALF), BF16),
            pltpu.VMEM((2, 3, 4, 4, Q, wide), BF16),
            pltpu.VMEM((2, 3, 2, 4, 4, Q, wide), BF16),
            pltpu.VMEM((2, 3, 4, Q, wide), BF16),
            pltpu.VMEM((2, 3, 2, 4, Q, wide), BF16),
            pltpu.VMEM((2, 3, 3, Q, wide), BF16),
            pltpu.VMEM((2, Q, HALF), BF16),
            pltpu.VMEM((Q, HALF), BF16),
            pltpu.VMEM((4, Q, D), BF16),
            dma((3,)),
            dma((3,)),
            dma((2, 3, 12)),
            dma((2, 3, 12)),
            dma((2, 3, 4)),
            dma((2, 3, 4)),
            dma((2,)),
            dma((2, 2)),
            dma((2,)),
            dma((2, 3, 4)),
            dma((2, 3, 4)),
            dma((2, 3, 15)),
            dma((2, 3, 15)),
            dma((2,)),
            dma((2,)),
            dma((3,)),
            dma((3,)),
        ],
        compiler_params=pltpu.CompilerParams(
            collective_id=0, has_side_effects=True, vmem_limit_bytes=VMEM_LIMIT
        ),
    )(part, hidden, gain, aux, gate_up, down)[0]


def rms_scale(inputs, gain):
    inputs = inputs.astype(F32)
    scaled = inputs * lax.rsqrt(jnp.mean(inputs * inputs, axis=-1, keepdims=True) + eps_norm)
    return (scaled * gain).astype(BF16)


def request_tables(new_lengths, prefix_lengths, row_count, cache_count):
    new_end = jnp.cumsum(new_lengths, dtype=jnp.int32)
    cache_end = jnp.cumsum(prefix_lengths, dtype=jnp.int32)
    token_index = jnp.arange(row_count, dtype=jnp.int32)
    cache_index = jnp.arange(cache_count, dtype=jnp.int32)
    token_request = jnp.sum(
        (token_index[:, None] >= new_end[None, :]).astype(jnp.int32), axis=1, dtype=jnp.int32
    )
    cache_request = jnp.sum(
        (cache_index[:, None] >= cache_end[None, :]).astype(jnp.int32), axis=1, dtype=jnp.int32
    )
    requests = new_lengths.shape[0]
    selector = token_request[:, None] == jnp.arange(requests, dtype=jnp.int32)[None, :]
    new_start = new_end - new_lengths
    offset = token_index - jnp.sum(
        jnp.where(selector, new_start[None, :], 0), axis=1, dtype=jnp.int32
    )
    position = offset + jnp.sum(
        jnp.where(selector, prefix_lengths[None, :], 0), axis=1, dtype=jnp.int32
    )
    return (token_request, cache_request, position)


def project_heads(normed, weight, gains, position, head_size):
    row_count = normed.shape[0]
    proj_width = weight.shape[2]
    full_width = proj_width * lax.axis_size("tp")
    by_member = jnp.transpose(weight, (1, 0, 2))
    projected = [
        jnp.dot(normed, by_member[m], preferred_element_type=F32) for m in range(3)
    ]
    squares = jnp.stack([jnp.sum(projected[m] * projected[m], axis=1) for m in range(2)], axis=1)
    totals = lax.psum(squares, "tp")
    inverse = lax.rsqrt(totals / full_width + eps_head)
    head_count = proj_width // head_size
    half_size = head_size // 2
    frequency = rope_base ** (-jnp.arange(half_size, dtype=F32) * 2.0 / head_size)
    angles = position.astype(F32)[:, None] * frequency[None, :]
    cosine = jnp.cos(angles)[:, None, :]
    sine_table = jnp.sin(angles)[:, None, :]
    outputs = []
    for member in range(2):
        member_rows = projected[member] * inverse[:, member : member + 1]
        portion = (member_rows * gains[member][None, :]).reshape(row_count, head_count, head_size)
        lower_half = portion[..., :half_size]
        upper_half = portion[..., half_size:]
        turned = jnp.concatenate(
            [
                lower_half * cosine - upper_half * sine_table,
                upper_half * cosine + lower_half * sine_table,
            ],
            axis=-1,
        )
        outputs.append(turned.reshape(row_count, proj_width).astype(BF16))
    outputs.append(projected[2].astype(BF16))
    return outputs


def attend(qkv, key_cache, value_cache, token_request, cache_request, head_size):
    row_count, proj_width = qkv[0].shape
    head_count = proj_width // head_size
    queries = qkv[0].reshape(row_count, head_count, head_size)
    key_rows = jnp.concatenate([key_cache, qkv[1]], axis=0).reshape(-1, head_count, head_size)
    value_rows = jnp.concatenate([value_cache, qkv[2]], axis=0).reshape(
        -1, head_count, head_size
    )
    scores = jnp.einsum(
        "qhd,khd->hqk", queries, key_rows, preferred_element_type=F32
    ) / math.sqrt(head_size)
    token_index = jnp.arange(row_count, dtype=jnp.int32)
    cache_ok = cache_request[None, :] == token_request[:, None]
    new_ok = (token_request[None, :] == token_request[:, None]) & (
        token_index[None, :] <= token_index[:, None]
    )
    allowed = jnp.concatenate([cache_ok, new_ok], axis=1)
    scores = jnp.where(allowed[None], scores, -1e30)
    row_max = jnp.max(scores, axis=-1, keepdims=True)
    weights = jnp.exp(scores - row_max)
    weights = (weights / jnp.sum(weights, axis=-1, keepdims=True)).astype(BF16)
    context = jnp.einsum("hqk,khd->qhd", weights, value_rows, preferred_element_type=F32)
    return context.reshape(row_count, proj_width).astype(BF16)


def weight_columns(expert_ids, expert_weights):
    experts = jnp.arange(NE, dtype=jnp.int32)[None, :]
    dense = jnp.zeros((expert_ids.shape[0], NE), F32)
    for k in range(expert_ids.shape[1]):
        dense = dense + jnp.where(expert_ids[:, k:k + 1] == experts, expert_weights[:, k:k + 1], 0.0)
    high = lax.reduce_precision(dense, 8, 7)
    return jnp.concatenate([high, dense - high], axis=1).astype(BF16)


def per_device(
    hidden_in,
    new_lengths,
    prefix_lengths,
    cache_keys,
    cache_values,
    attn_gain,
    w_qkv,
    norm_gains,
    w_out,
    moe_gain,
    expert_ids,
    expert_weights,
    w_gate_up,
    w_down,
    next_gain,
    next_qkv,
    next_norm_gains,
):
    row_count, model_width = hidden_in.shape
    cache_count = cache_keys.shape[0]
    token_request, cache_request, position = request_tables(
        new_lengths[0], prefix_lengths[0], row_count, cache_count
    )
    normed = rms_scale(hidden_in, attn_gain)
    qkv = project_heads(normed, w_qkv, norm_gains, position, HD)
    context = attend(qkv, cache_keys, cache_values, token_request, cache_request, HD)
    attn_part = jnp.dot(context, w_out, preferred_element_type=F32).astype(BF16)
    aux = weight_columns(expert_ids, expert_weights)
    hidden_out = moe(attn_part, hidden_in, moe_gain[None, :], aux, jnp.transpose(w_gate_up, (0, 2, 1, 3)), w_down)
    next_input = rms_scale(hidden_out, next_gain)
    next_out = project_heads(next_input, next_qkv, next_norm_gains, position, HD)
    return (hidden_out, jnp.stack(next_out, axis=1))


def solution(mesh):
    placed = (
        P("rep", None),
        P("rep", None),
        P("rep", None),
        P("rep", "tp"),
        P("rep", "tp"),
        P(),
        P(None, None, "tp"),
        P(None, "tp"),
        P("tp", None),
        P(),
        P("rep", None),
        P("rep", None),
        P("rep", None, None, "tp"),
        P("rep", "tp", None),
        P(),
        P(None, None, "tp"),
        P(None, "tp"),
    )
    return jax.shard_map(
        per_device,
        mesh=mesh,
        in_specs=placed,
        out_specs=(P("rep", None), P("rep", None, "tp")),
        check_vma=False,
    )
```

time: 374 us -> 199 us (0.53)
  waiting for transfers between devices: 206 us -> 0 us
  Pallas kernels: 0 us -> 135 us
  local copies, waits for them, and re-layouts: 61.2 us -> 10.8 us
  starting transfers between devices: 19.9 us -> 0 us
  other arithmetic: 27.7 us -> 12.1 us
  between operations: 14.6 us -> 1.11 us
    all_to_all x2 -> x0, waiting for transfers between devices: 137 us -> none  [the longest x1 72.6 us: per_device(): lax.all_to_all(produced, 'rep', split_axis=0, concat_axis=0, tiled=True)]
    pallas_call x0 -> x1, Pallas kernels: none -> 135 us  [moe(): pl.pallas_call(moe_kernel, name='moe', out_shape=(jax.ShapeDtypeStruct((R...]
    psum x2 -> x0, waiting for transfers between devices: 68.3 us -> none  [the longest x1 35.4 us: per_device(): lax.psum(attn_part.astype(jnp.bfloat16), 'tp').astype(jnp.float32)]
    all_to_all x2 -> x0, starting transfers between devices: 19.6 us -> none  [the longest x1 9.83 us: per_device(): lax.all_to_all(produced, 'rep', split_axis=0, concat_axis=0, tiled=True)]
    gather x2 -> x0, local copies, waits for them, and re-layouts: 19.5 us -> none  [the longest x1 12.4 us: per_device(): returned.reshape(expert_count * full_cap, model_width)[flat_slot]]
    unnamed x48 -> x45, local copies, waits for them, and re-layouts: 24.7 us -> 7.18 us
    reduce_sum x4 -> x0, other arithmetic: 7.72 us -> none  [the longest x1 7.32 us: per_device(): jnp.sum(picked.reshape(row_count, choose_count, model_width) * expert_wei...]
    slice x9 -> x4, local copies, waits for them, and re-layouts: 8.71 us -> 1.1 us  [the longest x2 0.69 us: project_heads(): upper_half = portion[..., half_size:]]
  transfers between devices with their start and end apart: 4 -> 0, of which waited for: 4 -> 0; matrix products, arithmetic and copies ran while one was open for 7% -> 0% of each run, Pallas kernels for 0% -> 0%
where the time goes in v2:
time: 199 us; the launch traced here: 197 us
  Pallas kernels  135 us (68%)
  matrix products  21.7 us (11%)
  blocking collectives  16.4 us (8%)
  other arithmetic  12.1 us (6%)
  local copies, waits for them, and re-layouts  10.8 us (5%)
    pallas_call x1, Pallas kernels, moe(): pl.pallas_call(moe_kernel, name='moe', out_shape=(jax.ShapeDtypeStruct((R...  135 us
    psum x2, blocking collectives, project_heads(): totals = lax.psum(squares, 'tp')  16.4 us
    dot_general x6, matrix products, project_heads(): jnp.dot(normed, by_member[m], preferred_element_type=F32)  13.9 us
    unnamed x45, local copies, waits for them, and re-layouts  7.18 us

profile of v2, /device:TPU:1, one launch (start us, length us, event | category | flops | bytes accessed | tf_op | source)
XLA Modules:
  0.0 197.5 jit_solution(971605286135167875)
XLA Ops:
  0.6 0.0 copy-start
  0.6 0.0 copy-start.2
  0.7 0.0 copy-start.12
  0.7 1.4 fusion.15
  2.1 2.3 %multiply_reduce_fusion.2 = (f32[128]{0:T(128)S(1)}, f32[128,512]{1,0:T(8,128)S(1)}) fusion(bf16[3,2048,512]{2,1,0:T(8,128)(2,1)} %bitcast.134, bf16[128,2048]{1,0:T(8,128)(2,1)} %hidden_ref.1, f32[2048]{0:T(1024)} %param.22, f32[128]{0:T(128)S(1)} %add_rsqrt_fusion.3), kind=kOutput, calls=%fused_computation.53 | convolution fusion | flops 269614976 | bytes 2892800 | tf_op jit(solution)/shard_map/dot_general | solution.py:559
  4.4 0.0 copy-start.7
  4.4 2.2 %multiply_reduce_fusion.3 = (f32[128]{0:T(128)S(1)}, f32[128,512]{1,0:T(8,128)S(1)}) fusion(bf16[3,2048,512]{2,1,0:T(8,128)(2,1)} %bitcast.135, bf16[128,2048]{1,0:T(8,128)(2,1)S(1)} %copy-done.2, f32[2048]{0:T(1024)S(1)} %copy-done.12, f32[128]{0:T(128)S(1)} %add_rsqrt_fusion.3), kind=kOutput, calls=%fused_computation.54 | convolution fusion | flops 269614976 | bytes 2892800 | tf_op jit(solution)/shard_map/dot_general | solution.py:559
  6.6 0.0 copy-start.14
  6.6 0.0 copy-start.11
  6.6 9.6 %psum.14 = f32[128,2]{0,1:T(2,128)S(1)} all-reduce(f32[128,2]{0,1:T(2,128)S(1)} %pad_maximum_fusion.7), channel_id=1, replica_groups=mesh['rep'=32,'tp'=4] {'tp'}, use_global_device_ids=true, to_apply=%region_7.8 | all-reduce | flops 256 | bytes 2048 | tf_op jit(solution)/shard_map/psum | solution.py:562
  16.2 0.1 multiply_multiply_fusion.2
  16.4 0.1 reshape.177
  16.5 0.2 fusion.45
  16.7 0.1 reshape.179
  16.8 0.2 fusion.46
  17.0 0.2 reduce-window.14
  17.2 0.1 convert_reduce_fusion.1
  17.2 0.1 select_reduce_fusion.1
  17.4 0.3 multiply_cosine_fusion
  17.7 0.8 subtract_convert_fusion.3
  18.5 0.1 pad_maximum_fusion.3
  18.6 0.1 copy.49
  18.8 0.0 copy-start.6
  18.8 1.5 copy.50
  20.3 1.1 pad_maximum_fusion.1
  21.4 0.2 reduce-window.13
  21.6 0.1 convert_reduce_fusion
  21.7 0.1 broadcast_compare_fusion
  21.8 0.1 fusion.27
  22.0 0.0 copy-start.3
  22.0 3.8 %fusion.49 = (f32[4,128]{1,0:T(4,128)S(1)}, f32[4,128,1152]{2,1,0:T(8,128)}) fusion(bf16[1152,4,128]{0,2,1:T(8,128)(2,1)} %bitcast.114, pred[128,1152]{1,0:T(8,128)(4,1)S(1)} %pad_add_fusion, bf16[128,4,64]{2,0,1:T(8,128)(2,1)} %get-tuple-element.11, bf16[128,4,64]{2,0,1:T(8,128)(2,1)S(1)} %copy-done.6), kind=kOutput, calls=%fused_computation.127 | convolution fusion | flops 153617536 | bytes 3819520 | tf_op jit(solution)/shard_map/sub | solution.py:607
  25.8 2.2 %fusion.11 = bf16[128,512]{1,0:T(8,128)(2,1)S(1)} fusion(bf16[3,2048,512]{2,1,0:T(8,128)(2,1)} %bitcast.136, bf16[128,2048]{1,0:T(8,128)(2,1)S(1)} %copy-done.3, f32[2048]{0:T(1024)S(1)} %copy-done.12, f32[128]{0:T(128)S(1)} %copy-done.16), kind=kOutput, calls=%fused_computation.27 | convolution fusion | flops 269549568 | bytes 2761216 | tf_op jit(solution)/shard_map/dot_general | solution.py:559
  28.0 0.1 pad_maximum_fusion
  28.1 1.4 copy.44
  29.5 2.8 %fusion.13 = bf16[4,128,128]{2,1,0:T(8,128)(2,1)S(1)} fusion(bf16[1152,4,128]{0,2,1:T(8,128)(2,1)} %bitcast.115, f32[4,128,1152]{2,1,0:T(8,128)} %get-tuple-element.59, f32[4,128]{1,0:T(4,128)S(1)} %get-tuple-element.58), kind=kOutput, calls=%fused_computation.29 | convolution fusion | flops 152240128 | bytes 3672064 | tf_op jit(solution)/shard_map/hqk,khd->qhd/dot_general | solution.py:609
  32.2 0.0 copy-start.8
  32.3 1.3 convolution_convert_fusion.part_ref
  33.6 0.3 reduce-precision_convert_fusion
  33.9 0.7 pad_maximum_fusion.6.aux_ref
  34.6 2.6 %copy.81 = bf16[2,2048,2,256]{3,1,2,0:T(8,128)(2,1)} copy(bf16[2,2048,2,256]{3,2,1,0:T(2,128)(2,1)S(1)} %copy-done.1) | data formatting | bytes 8388608 | tf_op args[12]
  37.3 135.4 %moe.1 = (bf16[128,2048]{1,0:T(8,128)(2,1)}, bf16[2,2,4,4,4,32,1152]{6,5,4,3,2,1,0:T(8,128)(2,1)}) custom-call(bf16[128,2048]{1,0:T(8,128)(2,1)} %convolution_convert_fusion.part_ref, bf16[128,2048]{1,0:T(8,128)(2,1)} %hidden_ref.1, f32[1,2048]{1,0:T(1,128)} %bitcast.126, bf16[128,128]{1,0:T(8,128)(2,1)} %pad_maximum_fusion.6.aux_ref, ...), custom_call_target="tpu_custom_call" | custom-call | tf_op jit(solution)/shard_map/moe/pallas_call | solution.py:470
  172.7 1.3 fusion.18
  174.0 2.3 %multiply_reduce_fusion = (f32[128]{0:T(128)S(1)}, f32[128,512]{1,0:T(8,128)S(1)}) fusion(bf16[3,2048,512]{2,1,0:T(8,128)(2,1)} %bitcast.137, bf16[128,2048]{1,0:T(8,128)(2,1)} %get-tuple-element.68, f32[2048]{0:T(1024)S(1)} %copy-done.13, f32[128]{0:T(128)S(1)} %add_rsqrt_fusion.2), kind=kOutput, calls=%fused_computation.45 | convolution fusion | flops 269614976 | bytes 2892800 | tf_op jit(solution)/shard_map/dot_general | solution.py:559
  176.3 2.8 %multiply_reduce_fusion.1 = (f32[128]{0:T(128)S(1)}, f32[128,512]{1,0:T(8,128)}) fusion(bf16[3,2048,512]{2,1,0:T(8,128)(2,1)} %bitcast.138, bf16[128,2048]{1,0:T(8,128)(2,1)S(1)} %copy-done.4, f32[2048]{0:T(1024)S(1)} %copy-done.13, f32[128]{0:T(128)S(1)} %add_rsqrt_fusion.2), kind=kOutput, calls=%fused_computation.46 | convolution fusion | flops 269614976 | bytes 2892800 | tf_op jit(solution)/shard_map/dot_general | solution.py:559
  179.1 6.9 %psum.15 = f32[128,2]{0,1:T(2,128)S(1)} all-reduce(f32[128,2]{0,1:T(2,128)S(1)} %pad_maximum_fusion.8), channel_id=1, replica_groups=mesh['rep'=32,'tp'=4] {'tp'}, use_global_device_ids=true, to_apply=%region_15.16 | all-reduce | flops 256 | bytes 2048 | tf_op jit(solution)/shard_map/psum | solution.py:562
  186.0 0.1 multiply_multiply_fusion
  186.1 0.1 copy.57
  186.3 0.1 copy.70
  186.4 0.8 copy.71
  187.3 1.0 multiply_multiply_fusion.1
  188.3 0.1 copy.53
  188.4 0.7 fusion.43
  189.1 0.1 copy.68
  189.3 1.0 copy.69
  190.3 1.8 subtract_convert_fusion.1
  192.1 0.1 pad_maximum_fusion.4
  192.2 0.1 copy.56
  192.3 0.1 copy.61
  192.4 1.1 pad_maximum_fusion.5
  193.5 0.1 copy.60
  193.7 0.1 copy.62
  193.8 2.1 %fusion.14 = bf16[128,1,512]{2,0,1:T(8,128)(2,1)S(1)} fusion(bf16[3,2048,512]{2,1,0:T(8,128)(2,1)} %bitcast.139, bf16[128,2048]{1,0:T(8,128)(2,1)S(1)} %copy-done.4, f32[2048]{0:T(1024)S(1)} %copy-done.13, f32[128]{0:T(128)S(1)} %copy-done.18), kind=kOutput, calls=%fused_computation.30 | convolution fusion | flops 269549568 | bytes 2761216 | tf_op jit(solution)/shard_map/dot_general | solution.py:559
  195.9 0.8 pad_maximum_fusion.2
  196.7 0.8 copy.83
  (46 shorter events, 0.2 us)
Async XLA Ops:
  0.6 31.6 %copy-start = (bf16[512,2048]{1,0:T(8,128)(2,1)S(1)}, bf16[512,2048]{1,0:T(8,128)(2,1)}, u32[]{:S(2)}) copy-start(bf16[512,2048]{1,0:T(8,128)(2,1)} %param.25) | copy-start | bytes 6291460
  0.6 3.8 %copy-start.2 = (bf16[128,2048]{1,0:T(8,128)(2,1)S(1)}, bf16[128,2048]{1,0:T(8,128)(2,1)}, u32[]{:S(2)}) copy-start(bf16[128,2048]{1,0:T(8,128)(2,1)} %hidden_ref.1) | copy-start | bytes 1572868
  0.7 3.8 %copy-start.12 = (f32[2048]{0:T(1024)S(1)}, f32[2048]{0:T(1024)}, u32[]{:S(2)}) copy-start(f32[2048]{0:T(1024)} %param.22) | copy-start | bytes 24580
  2.1 4.5 %copy-start.15 = (f32[128]{0:T(128)}, f32[128]{0:T(128)S(1)}, u32[]{:S(2)}) copy-start(f32[128]{0:T(128)S(1)} %add_rsqrt_fusion.3) | copy-start | bytes 1540
  4.4 11.8 %copy-start.7 = (f32[2,512]{1,0:T(2,128)S(1)}, f32[2,512]{1,0:T(2,128)}, u32[]{:S(2)}) copy-start(f32[2,512]{1,0:T(2,128)} %param.24) | copy-start | bytes 12292
  6.6 10.4 %copy-start.14 = (s32[1,4]{1,0:T(1,128)S(1)}, s32[1,4]{1,0:T(1,128)}, u32[]{:S(2)}) copy-start(s32[1,4]{1,0:T(1,128)} %param.18) | copy-start | bytes 52
  6.6 10.6 %copy-start.11 = (s32[1,4]{1,0:T(1,128)S(1)}, s32[1,4]{1,0:T(1,128)}, u32[]{:S(2)}) copy-start(s32[1,4]{1,0:T(1,128)} %param.19) | copy-start | bytes 52
  18.8 3.2 %copy-start.6 = (bf16[128,4,64]{2,0,1:T(8,128)(2,1)S(1)}, bf16[128,4,64]{2,0,1:T(8,128)(2,1)}, u32[]{:S(2)}) copy-start(bf16[128,4,64]{2,0,1:T(8,128)(2,1)} %get-tuple-element.10) | copy-start | bytes 196612
  22.0 3.8 %copy-start.3 = (bf16[128,2048]{1,0:T(8,128)(2,1)S(1)}, bf16[128,2048]{1,0:T(8,128)(2,1)}, u32[]{:S(2)}) copy-start(bf16[128,2048]{1,0:T(8,128)(2,1)} %hidden_ref.1) | copy-start | bytes 1572868
  22.0 3.8 %copy-start.16 = (f32[128]{0:T(128)S(1)}, f32[128]{0:T(128)}, u32[]{:S(2)}) copy-start(f32[128]{0:T(128)} %copy-done.15) | copy-start | bytes 1540
  25.8 2.2 %copy-start.5 = (bf16[1024,512]{1,0:T(8,128)(2,1)S(1)}, bf16[1024,512]{1,0:T(8,128)(2,1)}, u32[]{:S(2)}) copy-start(bf16[1024,512]{1,0:T(8,128)(2,1)} %param.21) | copy-start | bytes 3145732
  29.5 5.1 %copy-start.1 = (bf16[2,2048,2,256]{3,2,1,0:T(2,128)(2,1)S(1)}, bf16[2,2048,2,256]{3,2,1,0:T(2,128)(2,1)}, u32[]{:S(2)}) copy-start(bf16[2,2048,2,256]{3,2,1,0:T(2,128)(2,1)} %param.29) | copy-start | bytes 12582916
  32.2 1.3 copy-start.8
  32.3 1.3 copy-start.9
  37.3 136.7 %copy-start.13 = (f32[2048]{0:T(1024)S(1)}, f32[2048]{0:T(1024)}, u32[]{:S(2)}) copy-start(f32[2048]{0:T(1024)} %param.31) | copy-start | bytes 24580
  172.6 3.7 %copy-start.4 = (bf16[128,2048]{1,0:T(8,128)(2,1)S(1)}, bf16[128,2048]{1,0:T(8,128)(2,1)}, u32[]{:S(2)}) copy-start(bf16[128,2048]{1,0:T(8,128)(2,1)} %get-tuple-element.68) | copy-start | bytes 1572868
  174.0 5.2 %copy-start.17 = (f32[128]{0:T(128)}, f32[128]{0:T(128)S(1)}, u32[]{:S(2)}) copy-start(f32[128]{0:T(128)S(1)} %add_rsqrt_fusion.2) | copy-start | bytes 1540
  176.3 9.7 %copy-start.10 = (f32[2,512]{1,0:T(2,128)S(1)}, f32[2,512]{1,0:T(2,128)}, u32[]{:S(2)}) copy-start(f32[2,512]{1,0:T(2,128)} %param.33) | copy-start | bytes 12292
  188.4 5.4 %copy-start.18 = (f32[128]{0:T(128)S(1)}, f32[128]{0:T(128)}, u32[]{:S(2)}) copy-start(f32[128]{0:T(128)} %copy-done.17) | copy-start | bytes 1540

commit v3 on v2

--- a/solution.py
+++ b/solution.py
@@ -68,10 +68,10 @@
     return index + (pl.ds(*rows), pl.ds(*cols))
 
 
-def moe_kernel(part_ref, hidden_ref, gain_ref, aux_ref, gu_hbm, down_hbm, out_ref, g_ref,
-               inbox, own, mid, gu, down, gbuf, xs, ys, hot, scale, part, sib,
+def moe_kernel(normed_ref, stream_ref, aux_ref, gu_hbm, down_hbm, out_ref, g_ref,
+               own, gu, down, gbuf, xs, ys, hot, scale, part, sib,
                near, far, mnear, mfar, first, result, other, out,
-               tp_send, tp_recv, ag_send, ag_recv, share_send, share_recv, local_sem, load_sem, weight_sem,
+               ag_send, ag_recv, share_send, share_recv, local_sem, load_sem, weight_sem,
                sib_send, sib_recv, rs_send, rs_recv, swap_send, swap_recv, end_send, end_recv):
     coords, core = place()
     rep = lax.axis_index("rep")
@@ -90,26 +90,9 @@
         pending.append(copy)
         return copy
 
-    tp_copies = []
-    for k in (2, 1, 3):
-        peer = (y + k) % 4
-        tp_copies.append(push(
-            part_ref.at[pl.ds(pl.multiple_of(peer * Q, Q), Q), :], inbox.at[k - 1],
-            tp_send.at[k - 1], tp_recv.at[k - 1], device(moved(coords, 2, k), core)))
-    rows = pl.ds(pl.multiple_of(y * Q, Q), Q)
-    total = part_ref[rows, :].astype(F32)
-    for copy in tp_copies:
-        copy.wait_recv()
-    for k in range(3):
-        total = total + inbox[k].astype(F32)
-    stream = (hidden_ref[rows, :].astype(F32) + total).astype(BF16)
-    mid[...] = stream
-    wide = stream.astype(F32)
-    inverse = lax.rsqrt(jnp.mean(wide * wide, axis=-1, keepdims=True) + eps_norm)
-    normed = (wide * inverse * gain_ref[...]).astype(BF16)
     for h in range(2):
-        own[2 + h, :, pl.ds(0, HALF)] = normed[:, h * HALF:(h + 1) * HALF]
-        own[2 + h, :, pl.ds(HALF, AUX)] = aux_ref[rows, :]
+        own[2 + h, :, pl.ds(0, HALF)] = normed_ref[:, h * HALF:(h + 1) * HALF]
+        own[2 + h, :, pl.ds(HALF, AUX)] = aux_ref[pl.ds(pl.multiple_of(y * Q, Q), Q), :]
     own[core] = own[2 + core]
     swap = push(own.at[2 + (1 - core)], own.at[core], swap_send.at[0], swap_recv.at[0], sibling)
     return_own = swap
@@ -451,7 +434,7 @@
     for h in range(2):
         cols = pl.ds(h * HALF, HALF)
         term = jnp.where(core == h, result[core].astype(F32), other[...].astype(F32))
-        out[y, :, cols] = (mid[:, cols].astype(F32) + term).astype(BF16)
+        out[y, :, cols] = (stream_ref[:, cols].astype(F32) + term).astype(BF16)
     final = [
         push(out.at[y], out.at[y], end_send.at[k - 1], end_recv.at[k - 1], device(moved(coords, 2, k), core))
         for k in (2, 1, 3)
@@ -464,7 +447,7 @@
         out_ref[pl.ds(b * Q, Q), :] = out[b]
 
 
-def moe(part, hidden, gain, aux, gate_up, down):
+def moe(normed, stream, aux, gate_up, down):
     wide = max(w for _, w in REDUCE_PARTS)
     dma = pltpu.SemaphoreType.DMA
     return pl.pallas_call(
@@ -474,12 +457,10 @@
             jax.ShapeDtypeStruct((ROWS, D), BF16),
             jax.ShapeDtypeStruct((2, 2, 4, 4, 4, Q, WIDE), BF16),
         ),
-        in_specs=[pl.BlockSpec(memory_space=pltpu.VMEM)] * 4 + [pl.BlockSpec(memory_space=pltpu.HBM)] * 2,
+        in_specs=[pl.BlockSpec(memory_space=pltpu.VMEM)] * 3 + [pl.BlockSpec(memory_space=pltpu.HBM)] * 2,
         out_specs=(pl.BlockSpec(memory_space=pltpu.VMEM), pl.BlockSpec(memory_space=pltpu.HBM)),
         scratch_shapes=[
-            pltpu.VMEM((3, Q, D), BF16),
             pltpu.VMEM((4, Q, WIDE), BF16),
-            pltpu.VMEM((Q, D), BF16),
             pltpu.VMEM(gate_up.shape, BF16),
             pltpu.VMEM(down.shape, BF16),
             pltpu.VMEM((2, 2, 4, 4, Q, WIDE), BF16),
@@ -497,8 +478,6 @@
             pltpu.VMEM((2, Q, HALF), BF16),
             pltpu.VMEM((Q, HALF), BF16),
             pltpu.VMEM((4, Q, D), BF16),
-            dma((3,)),
-            dma((3,)),
             dma((2, 3, 12)),
             dma((2, 3, 12)),
             dma((2, 3, 4)),
@@ -516,98 +495,249 @@
             dma((3,)),
         ],
         compiler_params=pltpu.CompilerParams(
+            collective_id=1, has_side_effects=True, vmem_limit_bytes=VMEM_LIMIT
+        ),
+    )(normed, stream, aux, gate_up, down)[0]
+
+
+def greet_row(coords, core):
+    barrier = pltpu.get_barrier_semaphore()
+    for k in (1, 2, 3):
+        pl.semaphore_signal(barrier, inc=1, device_id=device(moved(coords, 2, k), core), device_id_type=MESH)
+    pl.semaphore_wait(barrier, 3)
+
+
+def send_to(src, dst, send_sem, recv_sem, peer):
+    copy = pltpu.make_async_remote_copy(
+        src_ref=src, dst_ref=dst, send_sem=send_sem, recv_sem=recv_sem, device_id=peer, device_id_type=MESH)
+    copy.start()
+    return copy
+
+
+def trade_squares(projected, sums, inbox, send, recv, coords, core):
+    lanes = lax.broadcasted_iota(jnp.int32, (ROWS, 128), 1)
+    packed = jnp.zeros((ROWS, 128), F32)
+    for m in range(2):
+        packed = jnp.where(lanes == m, jnp.sum(projected[m] * projected[m], axis=1, keepdims=True), packed)
+    sums[...] = packed.T[:8]
+    return [
+        send_to(sums, inbox.at[k - 1], send.at[k - 1], recv.at[k - 1], device(moved(coords, 2, k), core))
+        for k in (2, 1, 3)
+    ]
+
+
+def total_squares(copies, sums, inbox):
+    for copy in copies:
+        copy.wait_recv()
+    total = sums[...] + inbox[0] + inbox[1] + inbox[2]
+    inverse = lax.rsqrt(total / D + eps_head)
+    return jnp.concatenate([inverse, jnp.zeros((120, 128), F32)], axis=0).T
+
+
+def turn(rows, inverse, gains, cosine, sine):
+    heads = []
+    scaled = rows * inverse * gains
+    for h in range(rows.shape[1] // HD):
+        v = scaled[:, h * HD:(h + 1) * HD]
+        heads.append((v * cosine + pltpu.roll(v, HD // 2, 1) * sine).astype(BF16))
+    return heads
+
+
+def norm_rows(rows, gain):
+    wide = rows.astype(F32)
+    return (wide * lax.rsqrt(jnp.mean(wide * wide, axis=-1, keepdims=True) + eps_norm) * gain).astype(BF16)
+
+
+def attention_kernel(new_ref, prefix_ref, hidden_ref, gain_ref, w_hbm, head_gain_ref, keys_hbm, values_hbm, wo_hbm,
+                     moe_gain_ref, freq_ref, normed_ref, stream_ref, cos_ref, sin_ref,
+                     w, keys, values, wo, sums, inbox, part, half, full,
+                     w_sem, cache_sem, sum_send, sum_recv, send, recv):
+    coords, core = place()
+    y = coords[2]
+    fetch = [pltpu.make_async_copy(w_hbm.at[m], w.at[m], w_sem.at[m]) for m in range(3)]
+    fetch += [
+        pltpu.make_async_copy(keys_hbm, keys, cache_sem.at[0]),
+        pltpu.make_async_copy(values_hbm, values, cache_sem.at[1]),
+        pltpu.make_async_copy(wo_hbm, wo, cache_sem.at[2]),
+    ]
+    for copy in fetch:
+        copy.start()
+    greet_row(coords, core)
+    normed = norm_rows(hidden_ref[...], gain_ref[...])
+    projected = []
+    for m in range(2):
+        fetch[m].wait()
+        projected.append(jnp.dot(normed, w[m], preferred_element_type=F32))
+    copies = trade_squares(projected, sums, inbox, sum_send, sum_recv, coords, core)
+    fetch[2].wait()
+    fresh = jnp.dot(normed, w[2], preferred_element_type=F32).astype(BF16)
+
+    token = lax.broadcasted_iota(jnp.int32, (ROWS, 1), 0)
+    token_row = lax.broadcasted_iota(jnp.int32, (1, ROWS), 1)
+    cached = lax.broadcasted_iota(jnp.int32, (1, keys.shape[0]), 1)
+    position = token
+    request, request_row, cache_request = jnp.zeros_like(token), jnp.zeros_like(token_row), jnp.zeros_like(cached)
+    end, cache_end = 0, 0
+    for s in range(new_ref.shape[1]):
+        begin = end
+        end = end + new_ref[0, s]
+        cache_end = cache_end + prefix_ref[0, s]
+        inside = (token >= begin) & (token < end)
+        position = position + jnp.where(inside, prefix_ref[0, s] - begin, 0)
+        request = request + (token >= end).astype(jnp.int32)
+        request_row = request_row + (token_row >= end).astype(jnp.int32)
+        cache_request = cache_request + (cached >= cache_end).astype(jnp.int32)
+    angles = position.astype(F32) * freq_ref[...]
+    side = lax.broadcasted_iota(jnp.int32, (ROWS, HD), 1)
+    cosine = jnp.cos(angles)
+    sine = jnp.where(side < HD // 2, -1.0, 1.0) * jnp.sin(angles)
+    cos_ref[...] = cosine
+    sin_ref[...] = sine
+    cache_ok = cache_request == request
+    new_ok = (request_row == request) & (token_row <= token)
+    inverse = total_squares(copies, sums, inbox)
+    gains = head_gain_ref[...]
+    query_heads = turn(projected[0], inverse[:, 0:1], gains[0:1], cosine, sine)
+    key_heads = turn(projected[1], inverse[:, 1:2], gains[1:2], cosine, sine)
+    for n in (3, 4):
+        fetch[n].wait()
+    contract = (((1,), (1,)), ((), ()))
+    context = []
+    for h in range(len(query_heads)):
+        cols = pl.ds(h * HD, HD)
+        old = lax.dot_general(query_heads[h], keys[:, cols], contract, preferred_element_type=F32)
+        new = lax.dot_general(query_heads[h], key_heads[h], contract, preferred_element_type=F32)
+        old = jnp.where(cache_ok, old * (1.0 / math.sqrt(HD)), -1e30)
+        new = jnp.where(new_ok, new * (1.0 / math.sqrt(HD)), -1e30)
+        top = jnp.maximum(jnp.max(old, axis=1, keepdims=True), jnp.max(new, axis=1, keepdims=True))
+        old = jnp.exp(old - top)
+        new = jnp.exp(new - top)
+        total = jnp.sum(old, axis=1, keepdims=True) + jnp.sum(new, axis=1, keepdims=True)
+        scale = 1.0 / total
+        mixed = jnp.dot((old * scale).astype(BF16), values[:, cols], preferred_element_type=F32)
+        mixed = mixed + jnp.dot(
+            (new * scale).astype(BF16), fresh[:, h * HD:(h + 1) * HD], preferred_element_type=F32)
+        context.append(mixed.astype(BF16))
+    fetch[5].wait()
+    out = jnp.dot(jnp.concatenate(context, axis=1), wo[...], preferred_element_type=F32).astype(BF16)
+    for b in range(4):
+        part[b] = out[b * Q:(b + 1) * Q]
+    right, left = device(moved(coords, 2, 1), core), device(moved(coords, 2, 3), core)
+    low, high = pl.ds(0, 16), pl.ds(16, 16)
+    across, after, before = (y + 2) % 4, (y + 1) % 4, (y + 3) % 4
+    sends = [
+        send_to(part.at[across, low], half.at[low], send.at[0], recv.at[0], right),
+        send_to(part.at[across, high], half.at[high], send.at[1], recv.at[1], left),
+        send_to(part.at[after, high], full.at[0, high], send.at[2], recv.at[2], right),
+        send_to(part.at[before, low], full.at[1, low], send.at[3], recv.at[3], left),
+    ]
+    sends[0].wait_recv()
+    part[after, low] = part[after, low] + half[low]
+    sends.append(send_to(part.at[after, low], full.at[0, low], send.at[4], recv.at[4], right))
+    sends[1].wait_recv()
+    part[before, high] = part[before, high] + half[high]
+    sends.append(send_to(part.at[before, high], full.at[1, high], send.at[5], recv.at[5], left))
+    for copy in sends[2:]:
+        copy.wait_recv()
+    rows = pl.ds(pl.multiple_of(y * Q, Q), Q)
+    stream = hidden_ref[rows, :].astype(F32) + (
+        part[y].astype(F32) + full[0].astype(F32) + full[1].astype(F32))
+    stream = stream.astype(BF16)
+    stream_ref[...] = stream
+    normed_ref[...] = norm_rows(stream, moe_gain_ref[...])
+    for copy in copies + sends:
+        copy.wait_send()
+
+
+def frequencies():
+    half = HD // 2
+    frequency = rope_base ** (-jnp.arange(half, dtype=F32) * 2.0 / HD)
+    return jnp.concatenate([frequency, frequency])[None, :]
+
+
+def attention(new_lengths, prefix_lengths, hidden, gain, weight, head_gains, keys, values, w_out, moe_gain):
+    dma = pltpu.SemaphoreType.DMA
+    vmem, smem, hbm = (pl.BlockSpec(memory_space=s) for s in (pltpu.VMEM, pltpu.SMEM, pltpu.HBM))
+    return pl.pallas_call(
+        attention_kernel,
+        name="attention",
+        out_shape=(
+            jax.ShapeDtypeStruct((Q, D), BF16),
+            jax.ShapeDtypeStruct((Q, D), BF16),
+            jax.ShapeDtypeStruct((ROWS, HD), F32),
+            jax.ShapeDtypeStruct((ROWS, HD), F32),
+        ),
+        in_specs=[smem, smem, vmem, vmem, hbm, vmem, hbm, hbm, hbm, vmem, vmem],
+        out_specs=(vmem,) * 4,
+        scratch_shapes=[
+            pltpu.VMEM(weight.shape, BF16),
+            pltpu.VMEM(keys.shape, BF16),
+            pltpu.VMEM(values.shape, BF16),
+            pltpu.VMEM(w_out.shape, BF16),
+            pltpu.VMEM((8, 128), F32),
+            pltpu.VMEM((3, 8, 128), F32),
+            pltpu.VMEM((4, Q, D), BF16),
+            pltpu.VMEM((Q, D), BF16),
+            pltpu.VMEM((2, Q, D), BF16),
+            dma((3,)),
+            dma((3,)),
+            dma((3,)),
+            dma((3,)),
+            dma((6,)),
+            dma((6,)),
+        ],
+        compiler_params=pltpu.CompilerParams(
             collective_id=0, has_side_effects=True, vmem_limit_bytes=VMEM_LIMIT
         ),
-    )(part, hidden, gain, aux, gate_up, down)[0]
-
-
-def rms_scale(inputs, gain):
-    inputs = inputs.astype(F32)
-    scaled = inputs * lax.rsqrt(jnp.mean(inputs * inputs, axis=-1, keepdims=True) + eps_norm)
-    return (scaled * gain).astype(BF16)
-
-
-def request_tables(new_lengths, prefix_lengths, row_count, cache_count):
-    new_end = jnp.cumsum(new_lengths, dtype=jnp.int32)
-    cache_end = jnp.cumsum(prefix_lengths, dtype=jnp.int32)
-    token_index = jnp.arange(row_count, dtype=jnp.int32)
-    cache_index = jnp.arange(cache_count, dtype=jnp.int32)
-    token_request = jnp.sum(
-        (token_index[:, None] >= new_end[None, :]).astype(jnp.int32), axis=1, dtype=jnp.int32
-    )
-    cache_request = jnp.sum(
-        (cache_index[:, None] >= cache_end[None, :]).astype(jnp.int32), axis=1, dtype=jnp.int32
-    )
-    requests = new_lengths.shape[0]
-    selector = token_request[:, None] == jnp.arange(requests, dtype=jnp.int32)[None, :]
-    new_start = new_end - new_lengths
-    offset = token_index - jnp.sum(
-        jnp.where(selector, new_start[None, :], 0), axis=1, dtype=jnp.int32
-    )
-    position = offset + jnp.sum(
-        jnp.where(selector, prefix_lengths[None, :], 0), axis=1, dtype=jnp.int32
-    )
-    return (token_request, cache_request, position)
-
-
-def project_heads(normed, weight, gains, position, head_size):
-    row_count = normed.shape[0]
-    proj_width = weight.shape[2]
-    full_width = proj_width * lax.axis_size("tp")
-    by_member = jnp.transpose(weight, (1, 0, 2))
-    projected = [
-        jnp.dot(normed, by_member[m], preferred_element_type=F32) for m in range(3)
-    ]
-    squares = jnp.stack([jnp.sum(projected[m] * projected[m], axis=1) for m in range(2)], axis=1)
-    totals = lax.psum(squares, "tp")
-    inverse = lax.rsqrt(totals / full_width + eps_head)
-    head_count = proj_width // head_size
-    half_size = head_size // 2
-    frequency = rope_base ** (-jnp.arange(half_size, dtype=F32) * 2.0 / head_size)
-    angles = position.astype(F32)[:, None] * frequency[None, :]
-    cosine = jnp.cos(angles)[:, None, :]
-    sine_table = jnp.sin(angles)[:, None, :]
-    outputs = []
-    for member in range(2):
-        member_rows = projected[member] * inverse[:, member : member + 1]
-        portion = (member_rows * gains[member][None, :]).reshape(row_count, head_count, head_size)
-        lower_half = portion[..., :half_size]
-        upper_half = portion[..., half_size:]
-        turned = jnp.concatenate(
-            [
-                lower_half * cosine - upper_half * sine_table,
-                upper_half * cosine + lower_half * sine_table,
-            ],
-            axis=-1,
-        )
-        outputs.append(turned.reshape(row_count, proj_width).astype(BF16))
-    outputs.append(projected[2].astype(BF16))
-    return outputs
-
-
-def attend(qkv, key_cache, value_cache, token_request, cache_request, head_size):
-    row_count, proj_width = qkv[0].shape
-    head_count = proj_width // head_size
-    queries = qkv[0].reshape(row_count, head_count, head_size)
-    key_rows = jnp.concatenate([key_cache, qkv[1]], axis=0).reshape(-1, head_count, head_size)
-    value_rows = jnp.concatenate([value_cache, qkv[2]], axis=0).reshape(
-        -1, head_count, head_size
-    )
-    scores = jnp.einsum(
-        "qhd,khd->hqk", queries, key_rows, preferred_element_type=F32
-    ) / math.sqrt(head_size)
-    token_index = jnp.arange(row_count, dtype=jnp.int32)
-    cache_ok = cache_request[None, :] == token_request[:, None]
-    new_ok = (token_request[None, :] == token_request[:, None]) & (
-        token_index[None, :] <= token_index[:, None]
-    )
-    allowed = jnp.concatenate([cache_ok, new_ok], axis=1)
-    scores = jnp.where(allowed[None], scores, -1e30)
-    row_max = jnp.max(scores, axis=-1, keepdims=True)
-    weights = jnp.exp(scores - row_max)
-    weights = (weights / jnp.sum(weights, axis=-1, keepdims=True)).astype(BF16)
-    context = jnp.einsum("hqk,khd->qhd", weights, value_rows, preferred_element_type=F32)
-    return context.reshape(row_count, proj_width).astype(BF16)
+    )(new_lengths, prefix_lengths, hidden, gain, weight, head_gains, keys, values, w_out, moe_gain, frequencies())
+
+
+def next_kernel(hidden_ref, gain_ref, w_hbm, head_gain_ref, cos_ref, sin_ref, out_ref,
+                w, sums, inbox, w_sem, sum_send, sum_recv):
+    coords, core = place()
+    fetch = [pltpu.make_async_copy(w_hbm.at[m], w.at[m], w_sem.at[m]) for m in range(3)]
+    for copy in fetch:
+        copy.start()
+    greet_row(coords, core)
+    normed = norm_rows(hidden_ref[...], gain_ref[...])
+    projected = []
+    for m in range(2):
+        fetch[m].wait()
+        projected.append(jnp.dot(normed, w[m], preferred_element_type=F32))
+    copies = trade_squares(projected, sums, inbox, sum_send, sum_recv, coords, core)
+    fetch[2].wait()
+    out_ref[2] = jnp.dot(normed, w[2], preferred_element_type=F32).astype(BF16)
+    inverse = total_squares(copies, sums, inbox)
+    gains = head_gain_ref[...]
+    for m in range(2):
+        heads = turn(projected[m], inverse[:, m:m + 1], gains[m:m + 1], cos_ref[...], sin_ref[...])
+        for h, rows in enumerate(heads):
+            out_ref[m, :, pl.ds(h * HD, HD)] = rows
+    for copy in copies:
+        copy.wait_send()
+
+
+def next_heads(hidden, gain, weight, head_gains, cosine, sine):
+    dma = pltpu.SemaphoreType.DMA
+    vmem, hbm = (pl.BlockSpec(memory_space=s) for s in (pltpu.VMEM, pltpu.HBM))
+    return pl.pallas_call(
+        next_kernel,
+        name="next_heads",
+        out_shape=jax.ShapeDtypeStruct((3, ROWS, weight.shape[2]), BF16),
+        in_specs=[vmem, vmem, hbm, vmem, vmem, vmem],
+        out_specs=vmem,
+        scratch_shapes=[
+            pltpu.VMEM(weight.shape, BF16),
+            pltpu.VMEM((8, 128), F32),
+            pltpu.VMEM((3, 8, 128), F32),
+            dma((3,)),
+            dma((3,)),
+            dma((3,)),
+        ],
+        compiler_params=pltpu.CompilerParams(
+            collective_id=2, has_side_effects=True, vmem_limit_bytes=VMEM_LIMIT
+        ),
+    )(hidden, gain, weight, head_gains, cosine, sine)
 
 
 def weight_columns(expert_ids, expert_weights):
@@ -638,20 +768,15 @@
     next_qkv,
     next_norm_gains,
 ):
-    row_count, model_width = hidden_in.shape
-    cache_count = cache_keys.shape[0]
-    token_request, cache_request, position = request_tables(
-        new_lengths[0], prefix_lengths[0], row_count, cache_count
-    )
-    normed = rms_scale(hidden_in, attn_gain)
-    qkv = project_heads(normed, w_qkv, norm_gains, position, HD)
-    context = attend(qkv, cache_keys, cache_values, token_request, cache_request, HD)
-    attn_part = jnp.dot(context, w_out, preferred_element_type=F32).astype(BF16)
+    by_member = (1, 0, 2)
+    normed, stream, cosine, sine = attention(
+        new_lengths, prefix_lengths, hidden_in, attn_gain[None, :], jnp.transpose(w_qkv, by_member), norm_gains,
+        cache_keys, cache_values, w_out, moe_gain[None, :])
     aux = weight_columns(expert_ids, expert_weights)
-    hidden_out = moe(attn_part, hidden_in, moe_gain[None, :], aux, jnp.transpose(w_gate_up, (0, 2, 1, 3)), w_down)
-    next_input = rms_scale(hidden_out, next_gain)
-    next_out = project_heads(next_input, next_qkv, next_norm_gains, position, HD)
-    return (hidden_out, jnp.stack(next_out, axis=1))
+    hidden_out = moe(normed, stream, aux, jnp.transpose(w_gate_up, (0, 2, 1, 3)), w_down)
+    next_out = next_heads(
+        hidden_out, next_gain[None, :], jnp.transpose(next_qkv, by_member), next_norm_gains, cosine, sine)
+    return (hidden_out, jnp.transpose(next_out, by_member))
 
 
 def solution(mesh):

time: 199 us -> 169 us (0.85)
  Pallas kernels: 135 us -> 157 us
  matrix products: 21.7 us -> 0 us
  blocking collectives: 16.4 us -> 0 us
  other arithmetic: 12.1 us -> 1.64 us
    pallas_call x0 -> x2, Pallas kernels: none -> 26.4 us  [the longest x1 18.8 us: attention(): pl.pallas_call(attention_kernel, name='attention', out_shape=(jax.ShapeDt...]
    dot_general x8 -> x0, matrix products: 17.9 us -> none  [the longest x6 13.9 us: project_heads(): jnp.dot(normed, by_member[m], preferred_element_type=F32)]
    psum x2 -> x0, blocking collectives: 16.4 us -> none  [project_heads(): totals = lax.psum(squares, 'tp')]
    pallas_call x1, Pallas kernels: 135 us -> 130 us  [moe(): pl.pallas_call(moe_kernel, name='moe', out_shape=(jax.ShapeDtypeStruct((R...]
    sub x1 -> x0, matrix products: 3.82 us -> none  [attend(): weights = jnp.exp(scores - row_max)]
    another operation x8 -> x1, other arithmetic: 4.12 us -> 0.34 us
    reduce_sum x5 -> x0, other arithmetic: 2.93 us -> none  [the longest x2 2.67 us: rms_scale(): jnp.mean(inputs * inputs, axis=-1, keepdims=True) + eps_norm]
    concatenate x6 -> x0, other arithmetic: 2.51 us -> none  [the longest x3 1.3 us: project_heads(): jnp.concatenate([lower_half * cosine - upper_half * sine_table, upper_hal...]
where the time goes in v3:
time: 169 us; the launch traced here: 168 us
  Pallas kernels  157 us (93%)
  local copies, waits for them, and re-layouts  9.28 us (5%)
    pallas_call x1, Pallas kernels, moe(): pl.pallas_call(moe_kernel, name='moe', out_shape=(jax.ShapeDtypeStruct((R...  130 us
    pallas_call x1, Pallas kernels, attention(): pl.pallas_call(attention_kernel, name='attention', out_shape=(jax.ShapeDt...  18.8 us
    pallas_call x1, Pallas kernels, next_heads(): pl.pallas_call(next_kernel, name='next_heads', out_shape=jax.ShapeDtypeSt...  7.58 us
    unnamed x5, local copies, waits for them, and re-layouts  7.32 us

profile of v3, /device:TPU:1, one launch (start us, length us, event | category | flops | bytes accessed | tf_op | source)
XLA Modules:
  0.0 168.2 jit_solution(10452927738591350753)
XLA Ops:
  0.6 0.6 maximum_bitcast_fusion.freq_ref
  1.2 1.0 slice_bitcast_fusion.15
  2.2 1.0 slice_bitcast_fusion.14
  3.2 0.3 reduce-precision_convert_fusion
  3.5 0.7 pad_maximum_fusion.aux_ref
  4.2 18.8 %attention.1 = (bf16[32,2048]{1,0:T(8,128)(2,1)}, bf16[32,2048]{1,0:T(8,128)(2,1)}, f32[128,128]{1,0:T(8,128)}, f32[128,128]{1,0:T(8,128)}) custom-call(s32[1,4]{1,0:T(1,128)} %new_ref.1, s32[1,4]{1,0:T(1,128)} %prefix_ref.1, bf16[128,2048]{1,0:T(8,128)(2,1)} %hidden_ref.1, f32[1,2048]{1,0:T(1,128)} %bitcast.47, bf16[3,2048,512]{2,1,0:T(8,128)(2,1)} %bitcast.45, ...), custom_call_target="tpu_custom_call" | custom-call | tf_op jit(solution)/shard_map/attention/pallas_call | solution.py:661
  23.1 4.8 %copy.21 = bf16[2,2048,2,256]{3,1,2,0:T(8,128)(2,1)} copy(bf16[2,2048,2,256]{3,2,1,0:T(2,128)(2,1)} %param.29) | data formatting | bytes 8388608 | tf_op args[12]
  27.8 130.2 %moe.1 = (bf16[128,2048]{1,0:T(8,128)(2,1)}, bf16[2,2,4,4,4,32,1152]{6,5,4,3,2,1,0:T(8,128)(2,1)}) custom-call(bf16[32,2048]{1,0:T(8,128)(2,1)} %get-tuple-element.7.normed_ref, bf16[32,2048]{1,0:T(8,128)(2,1)} %get-tuple-element.8.stream_ref, bf16[128,128]{1,0:T(8,128)(2,1)} %pad_maximum_fusion.aux_ref, bf16[2,2,2048,256]{3,2,1,0:T(8,128)(2,1)} %bitcast.43, ...), custom_call_target="tpu_custom_call" | custom-call | tf_op jit(solution)/shard_map/moe/pallas_call | solution.py:453
  158.1 0.0 copy-start
  158.1 7.6 %next_heads.1 = bf16[3,128,512]{2,1,0:T(8,128)(2,1)} custom-call(bf16[128,2048]{1,0:T(8,128)(2,1)} %get-tuple-element.32.hidden_ref, f32[1,2048]{1,0:T(1,128)} %bitcast.49, bf16[3,2048,512]{2,1,0:T(8,128)(2,1)} %bitcast.44, f32[2,512]{1,0:T(2,128)} %head_gain_ref.3, f32[128,128]{1,0:T(8,128)} %get-tuple-element.10.cos_ref, f32[128,128]{1,0:T(8,128)} %get-tuple-element.11.sin_ref), custom_call_target="tpu_custom_call" | custom-call | tf_op jit(solution)/shard_map/next_heads/pallas_call | solution.py:723
  165.7 0.0 copy-done
  165.7 0.8 copy.24
  166.5 1.8 %copy.25 = bf16[128,3,512]{2,0,1:T(8,128)(2,1)} copy(bf16[128,3,512]{2,0,1:T(8,128)(2,1)} %bitcast.46) | data formatting | bytes 786432
  (1 shorter events, 0.0 us)
Async XLA Ops:
  158.1 7.6 %copy-start = (bf16[128,2048]{1,0:T(8,128)(2,1)S(1)}, bf16[128,2048]{1,0:T(8,128)(2,1)}, u32[]{:S(2)}) copy-start(bf16[128,2048]{1,0:T(8,128)(2,1)} %get-tuple-element.32.hidden_ref) | copy-start | bytes 1572868
